TPU v7x, 256 devices: a whole 4x4x8 slice. The times are simulated.
256 devices in a mesh: seq: 32 (over z, y), head: 4 (over x), dp: 2 (over core).
Axes of the slice: x: 4, y: 4, z: 8, core: 2. Of those that a mesh axis runs over, the one named last changes fastest.
Arguments:
- x_in: bfloat16 [16384, 8192], P(('dp', 'seq'), 'head'), parts along dimension 0, as said below
- bc_in: bfloat16 [16384, 2048], P(('dp', 'seq'), 'head'), parts along dimension 0, may hold values from -6 to 6
- z_in: bfloat16 [16384, 8192], P(('dp', 'seq'), 'head'), parts along dimension 0, may hold values from -6 to 6
- dt_raw: float32 [16384, 128], P(('dp', 'seq'), 'head'), parts along dimension 0, as said below
- dt_bias: float32 [128], P('head'), as said below
- a_log: float32 [128], P('head'), as said below
- d_skip: float32 [128], P('head'), may hold values from 0.5 to 1.5
- conv_x: float32 [4, 8192], P(None, 'head'), may hold values from -3 to 3
- conv_bc: float32 [4, 2048], P(None, 'head'), may hold values from -3 to 3
- norm_gain: float32 [8192], P('head'), may hold values from 0.1 to 1.9
- out_weight: bfloat16 [8192, 4096], P('head', 'seq'), may hold values from -0.125 to 0.125
Outputs:
- layer_out: bfloat16 [16384, 4096], P(('dp', 'seq'), 'head'), parts along dimension 0
There are 2 independent parts, one for each index of `dp`. A program takes and returns all parts, laid end to end along the dimension named above; an argument that names none is the same for every part. Nothing has to cross between parts.
Inputs may be any that keep to these rules, and one draw needn't show every extreme that they name: `x_in`: finite values. `dt_raw`: finite values. `dt_bias`: finite values. `a_log`: finite values.
All inputs are finite; a program needn't handle non-finite values.
Results may differ from a plain program's by a relative error of at most 0.0051.
Values may be sent and summed in bfloat16 or wider, within the bound.
No kernel may reach another device: no remote copies, remote signals or barrier semaphores. Data moves between devices by JAX's collectives and lax.ppermute only.
A program may use at most 192 MiB of HBM per device.

v0:
```python
import jax
import jax.numpy as jnp
from jax import lax
from jax.sharding import PartitionSpec as P

H = 128
P_SIZE = 64
N = 128
BLOCK = 256
CONV = 4


epsilon = 1e-05


def from_behind(block, axis, distance):
    devices = range(lax.axis_size(axis))
    route = [(i - distance, i) for i in devices if i - distance in devices]
    return lax.ppermute(block, axis, route)


def entering(value, axis, join, neutral):
    count, mine = (lax.axis_size(axis), lax.axis_index(axis))
    pieces = jax.tree.map(lambda part: lax.all_gather(part, axis), value)
    total = jax.tree.map(
        lambda part, zero: jnp.full_like(part, 0) + jnp.asarray(zero, part.dtype), value, neutral
    )

    def lap(position, total):
        longer = join(total, jax.tree.map(lambda part: part[position], pieces))
        return jax.tree.map(lambda new, old: jnp.where(position < mine, new, old), longer, total)

    return lax.fori_loop(0, count - 1, lap, total)


def conv_with(before, current, weight):
    height = current.shape[0]
    joined = jnp.concatenate([before, current], axis=0).astype(jnp.float32)
    summed = jnp.zeros(current.shape, jnp.float32)
    for offset in range(CONV):
        summed = summed + weight[offset][None, :] * joined[offset : offset + height]
    return summed


def combine_carry(earlier, later):
    return (earlier[0] * later[0], later[0][:, None, None] * earlier[1] + later[1])


def shards(
    x_in, bc_in, z_in, dt_raw, dt_bias, a_log, d_skip, conv_x, conv_bc, norm_gain, out_weight
):
    height = x_in.shape[0]
    heads = dt_raw.shape[1]
    local_width = x_in.shape[1]
    nearby_groups = bc_in.shape[1] // (2 * N)
    per_group = heads // nearby_groups
    tails = from_behind((x_in[height - (CONV - 1) :], bc_in[height - (CONV - 1) :]), "seq", 1)
    input_convolved = jax.nn.silu(conv_with(tails[0], x_in, conv_x)).astype(jnp.bfloat16)
    bc_conv = jax.nn.silu(conv_with(tails[1], bc_in, conv_bc)).astype(jnp.bfloat16)
    step_sizes = jax.nn.softplus(dt_raw + dt_bias[None, :])
    log_decay = -jnp.exp(a_log)[None, :] * step_sizes
    blocks = height // BLOCK
    x_blocks = input_convolved.reshape(blocks, BLOCK, heads, P_SIZE)
    bc_blocks = bc_conv.reshape(blocks, BLOCK, nearby_groups, 2, N)
    b_mat = bc_blocks[:, :, :, 0]
    c_mat = bc_blocks[:, :, :, 1]
    running = jnp.cumsum(log_decay.reshape(blocks, BLOCK, heads), axis=1)
    step_blocks = step_sizes.reshape(blocks, BLOCK, heads)
    places = jnp.arange(BLOCK, dtype=jnp.int32)
    lower = places[:, None] >= places[None, :]

    def inside(input_rows):
        x_here, b_here, c_here, run_here, step_here = input_rows
        scores = jnp.einsum("ign,jgn->gij", c_here, b_here, preferred_element_type=jnp.float32)
        run_heads = run_here.T.reshape(nearby_groups, per_group, BLOCK)
        step_heads = step_here.T.reshape(nearby_groups, per_group, BLOCK)
        spread = run_heads[:, :, :, None] - run_heads[:, :, None, :]
        spread = jnp.where(lower[None, None], spread, -jnp.inf)
        mixing = (scores[:, None] * jnp.exp(spread) * step_heads[:, :, None, :]).astype(
            jnp.bfloat16
        )
        mixing = mixing.reshape(heads, BLOCK, BLOCK)
        within = jnp.einsum("hij,jhp->ihp", mixing, x_here, preferred_element_type=jnp.float32)
        until_finish = jnp.exp(run_here[-1:] - run_here) * step_here
        b_heads = jnp.repeat(b_here.astype(jnp.float32), per_group, axis=1)
        weighted_b = (b_heads * until_finish[:, :, None]).astype(jnp.bfloat16)
        fresh = jnp.einsum("jhn,jhp->hnp", weighted_b, x_here, preferred_element_type=jnp.float32)
        return (within, fresh)

    within, fresh = lax.map(inside, (x_blocks, b_mat, c_mat, running, step_blocks))
    since_beginning = (
        jnp.repeat(c_mat.astype(jnp.float32), per_group, axis=2) * jnp.exp(running)[..., None]
    )
    block_decay = running[:, -1, :]
    state = jnp.zeros((heads, N, P_SIZE), jnp.float32)
    prefix = jnp.zeros((heads,), jnp.float32)
    starts = [state]
    offsets = [prefix]
    state = jnp.exp(block_decay[0])[:, None, None] * state + fresh[0]
    prefix = block_decay[0]
    start_states = jnp.stack(starts)
    start_logs = jnp.stack(offsets)
    unused, incoming = entering(
        (jnp.exp(prefix), state),
        "seq",
        combine_carry,
        (jnp.ones((heads,), jnp.float32), jnp.zeros((heads, N, P_SIZE), jnp.float32)),
    )
    full_starts = start_states + jnp.exp(start_logs)[:, :, None, None] * incoming[None]
    across = jnp.einsum(
        "cihn,chnp->cihp", since_beginning, full_starts, precision=lax.Precision.HIGHEST
    )
    mixed = within + across + d_skip[None, None, :, None] * x_blocks.astype(jnp.float32)
    mixed = mixed.reshape(height, local_width)
    gated = mixed * jax.nn.silu(z_in.astype(jnp.float32))
    square_sums = lax.psum(jnp.sum(gated * gated, axis=1), "head")
    normed = (
        gated * lax.rsqrt(square_sums / (H * P_SIZE) + epsilon)[:, None] * norm_gain[None, :]
    ).astype(jnp.bfloat16)
    terms = jnp.dot(
        normed,
        lax.all_gather(out_weight, "seq", axis=1, tiled=True),
        preferred_element_type=jnp.float32,
    )
    return lax.psum_scatter(terms, "head", scatter_dimension=1, tiled=True).astype(jnp.bfloat16)


def solution(mesh):
    placed = (
        P(("dp", "seq"), "head"),
        P(("dp", "seq"), "head"),
        P(("dp", "seq"), "head"),
        P(("dp", "seq"), "head"),
        P("head"),
        P("head"),
        P("head"),
        P(None, "head"),
        P(None, "head"),
        P("head"),
        P("head", "seq"),
    )
    return jax.shard_map(
        shards, mesh=mesh, in_specs=placed, out_specs=P(("dp", "seq"), "head"), check_vma=False
    )
```

profile of v0, /device:TPU:1, one launch (start us, length us, event | category | flops | bytes accessed | tf_op | source)
XLA Modules:
  0.0 516.0 jit_solution(12045044107873377527)
XLA Ops:
  8.2 4.7 collective-permute-start.1
  35.7 39.3 %all-gather = f32[32,1,32]{2,1,0:T(1,128)S(1)} all-gather(f32[1,1,32]{2,1,0:T(1,128)S(1)} %get-tuple-element.189), channel_id=2, replica_groups=mesh['seq'=32,'head'=4,'dp'=2] {'seq'}, dimensions={0}, use_global_device_ids=true | all-gather | bytes 4224 | tf_op jit(solution)/shard_map/all_gather | solution.py:24
  75.2 3.3 bitcast_multiply_fusion.1
  83.7 187.5 %all-gather.7.cloned.1.call-done = f32[1024,128,64]{1,2,0:T(8,128)} async-done(((f32[32,128,64]{1,2,0:T(8,128)}), f32[1024,128,64]{1,2,0:T(8,128)}) %all-gather.7.cloned.1.call-update) | async-done | bytes 33554448 | tf_op jit(solution)/shard_map/all_gather | solution.py:24
  271.3 160.6 %while.9 = (s32[]{:T(128)}, f32[32,128,64]{2,1,0:T(8,128)}, s32[]{:T(128)}, f32[32,32]{1,0:T(8,128)S(1)}, f32[32,32,128,64]{2,3,1,0:T(8,128)}, /*index=5*/s32[]{:T(128)}, s32[]{:T(128)}) while((s32[]{:T(128)}, f32[32,128,64]{2,1,0:T(8,128)}, s32[]{:T(128)}, f32[32,32]{1,0:T(8,128)S(1)}, f32[32,32,128,64]{2,3,1,0:T(8,128)}, ...), condition=%wide.region_3.4_spmd.clone, body=%wide.region_2.3_spmd.clone.sunk | while | flops 1048580 | bytes 7340521 | solution.py:33
  282.0 3.3 fusion.40
  292.5 3.3 fusion.40
  297.8 3.3 fusion.40
  313.5 3.3 fusion.40
  334.3 3.3 fusion.40
  339.6 3.3 fusion.40
  350.1 3.3 fusion.40
  360.5 3.4 fusion.40
  365.9 3.3 fusion.40
  371.1 3.3 fusion.40
  376.3 3.3 fusion.40
  381.6 3.3 fusion.40
  386.9 3.3 fusion.40
  397.4 3.3 fusion.40
  407.8 3.3 fusion.40
  431.9 7.5 %fusion.31 = f32[32,64,256]{2,1,0:T(8,128)S(1)} fusion(f32[32,128,64]{2,1,0:T(8,128)} %get-tuple-element.126, f32[256,32,128]{2,0,1:T(8,128)} %bitcast_multiply_fusion.1), kind=kOutput, calls=%fused_computation.70 | convolution fusion | flops 805306368 | bytes 7340032 | tf_op jit(solution)/shard_map/cihn,chnp->cihp/dot_general | solution.py:110
  441.4 8.4 %psum.7 = f32[256]{0:T(256)S(1)} all-reduce(f32[256]{0:T(256)S(1)} %get-tuple-element.180), channel_id=1, replica_groups=mesh['seq'=32,'head'=4,'dp'=2] {'head'}, use_global_device_ids=true, to_apply=%region_5.6 | all-reduce | flops 256 | bytes 2048 | tf_op jit(solution)/shard_map/psum | solution.py:116
  449.8 10.3 %fusion.12 = f32[256,4096]{1,0:T(8,128)} fusion(bf16[2048,4096]{1,0:T(8,128)(2,1)} %all-gather.5.cloned.1.call-done, f32[256,2048]{0,1:T(8,128)S(1)} %get-tuple-element.181, f32[2048]{0:T(1024)S(1)} %copy-done.7, f32[256]{0:T(256)S(1)} %add_rsqrt_fusion), kind=kOutput, calls=%fused_computation.31 | convolution fusion | flops 4296540160 | bytes 23077888 | tf_op jit(solution)/shard_map/dot_general | solution.py:120
  460.1 47.3 %reduce-scatter.2.cloned.1.call-done = f32[256,1024]{1,0:T(8,128)} async-done(((f32[256,4096]{1,0:T(8,128)}), f32[256,1024]{1,0:T(8,128)}) %reduce-scatter.2.cloned.1.call-update) | async-done | bytes 1048592 | tf_op jit(solution)/shard_map/reduce_scatter | solution.py:125
  (188 shorter events, 143.9 us)
Async XLA Ops:
  6.5 14.9 %copy-start.6 = (bf16[256,512]{1,0:T(8,128)(2,1)S(1)}, bf16[256,512]{1,0:T(8,128)(2,1)}, u32[]{:S(2)}) copy-start(bf16[256,512]{1,0:T(8,128)(2,1)} %param.14) | copy-start | bytes 786436
  6.5 15.0 %copy-start.4 = (bf16[256,2048]{1,0:T(8,128)(2,1)S(1)}, bf16[256,2048]{1,0:T(8,128)(2,1)}, u32[]{:S(2)}) copy-start(bf16[256,2048]{1,0:T(8,128)(2,1)} %param.13) | copy-start | bytes 3145732
  6.5 14.8 %copy-start.9 = (f32[4,512]{1,0:T(4,128)S(1)}, f32[4,512]{1,0:T(4,128)}, u32[]{:S(2)}) copy-start(f32[4,512]{1,0:T(4,128)} %param.21) | copy-start | bytes 24580
  6.5 14.8 %copy-start.8 = (f32[4,2048]{1,0:T(4,128)S(1)}, f32[4,2048]{1,0:T(4,128)}, u32[]{:S(2)}) copy-start(f32[4,2048]{1,0:T(4,128)} %param.20) | copy-start | bytes 98308
  6.5 264.8 %all-gather.7.cloned.1.call-start = ((), (), s32[]{:S(2)}) async-start(), calls=%async_computation.3 | async-start | bytes 34603008 | tf_op jit(solution)/shard_map/all_gather | solution.py:24
  8.2 14.0 %collective-permute-start.1 = (bf16[3,512]{0,1:T(8,128)(2,1)}, bf16[3,512]{0,1:T(8,128)(2,1)}, u32[]{:S(2)}, u32[]{:S(2)}) collective-permute-start(bf16[3,512]{0,1:T(8,128)(2,1)} %copy.66), channel_id=1, source_target_pairs={{0,8},{8,16},{16,24},{24,32},{32,40},{40,48},{48,56},{56,64},{64,7... | collective-permute-start | bytes 9224 | tf_op jit(solution)/shard_map/ppermute | solution.py:19
  14.7 13.2 %collective-permute-start = (bf16[3,2048]{0,1:T(8,128)(2,1)}, bf16[3,2048]{0,1:T(8,128)(2,1)S(1)}, u32[]{:S(2)}, u32[]{:S(2)}) collective-permute-start(bf16[3,2048]{0,1:T(8,128)(2,1)} %copy.64), channel_id=1, source_target_pairs={{0,8},{8,16},{16,24},{24,32},{32,40},{40,48},{48,56},{56,64},{64,7... | collective-permute-start | bytes 36872 | tf_op jit(solution)/shard_map/ppermute | solution.py:19
  31.7 49.3 %copy-start = (bf16[256,2048]{0,1:T(8,128)(2,1)}, bf16[256,2048]{0,1:T(8,128)(2,1)S(1)}, u32[]{:S(2)}) copy-start(bf16[256,2048]{0,1:T(8,128)(2,1)S(1)} %multiply_convert_fusion.1) | copy-start | bytes 3145732
  31.7 2.6 copy-start.5
  33.3 416.5 %all-gather.5.cloned.1.call-start = ((), (), s32[]{:S(2)}) async-start(), calls=%async_computation.1 | async-start | bytes 17301504 | tf_op jit(solution)/shard_map/all_gather | solution.py:122
  34.1 473.3 %reduce-scatter.2.cloned.1.call-start = ((), (), s32[]{:S(2)}) async-start(), calls=%async_computation.2 | async-start | bytes 5242880 | tf_op jit(solution)/shard_map/reduce_scatter | solution.py:125
  431.9 7.5 %copy-start.1 = (bf16[256,2048]{0,1:T(8,128)(2,1)S(1)}, bf16[256,2048]{0,1:T(8,128)(2,1)}, u32[]{:S(2)}) copy-start(bf16[256,2048]{0,1:T(8,128)(2,1)} %copy-done) | copy-start | bytes 3145732
  431.9 7.5 %copy-start.2 = (f32[32,64,256]{2,1,0:T(8,128)S(1)}, f32[32,64,256]{2,1,0:T(8,128)}, u32[]{:S(2)}) copy-start(f32[32,64,256]{2,1,0:T(8,128)} %fusion.30) | copy-start | bytes 6291460
  431.9 7.5 %copy-start.10 = (f32[32]{0:T(128)S(1)}, f32[32]{0:T(128)}, u32[]{:S(2)}) copy-start(f32[32]{0:T(128)} %param.19) | copy-start | bytes 388
  439.4 1.2 copy-start.3
  440.7 9.1 %copy-start.7 = (f32[2048]{0:T(1024)S(1)}, f32[2048]{0:T(1024)}, u32[]{:S(2)}) copy-start(f32[2048]{0:T(1024)} %param.22) | copy-start | bytes 24580
Sparse Core Ops, SparseCore 0:
  33.4 237.8 all-gather.6
  273.8 143.4 all-gather.4
  460.3 47.1 reduce-scatter.1
where the time goes:
time: 519 us; the launch traced here: 516 us
  waiting for transfers between devices  238 us (46%)
  other arithmetic  119 us (23%)
  local copies, waits for them, and re-layouts  67.4 us (13%)
  blocking collectives  47.6 us (9%)
  matrix products  22.3 us (4%)
  between operations  13.4 us (3%)
  starting transfers between devices  7.36 us (1%)
    all_gather x1, waiting for transfers between devices, entering(): pieces = jax.tree.map(lambda part: lax.all_gather(part, axis), value)  188 us
    select_n x31, other arithmetic, lap(): jnp.where(position < mine, new, old)  100 us
    dynamic_slice x62, local copies, waits for them, and re-layouts, lap(): longer = join(total, jax.tree.map(lambda part: part[position], pieces))  59.2 us
    reduce_scatter x1, waiting for transfers between devices, shards(): lax.psum_scatter(terms, 'head', scatter_dimension=1, tiled=True)  47.3 us
    all_gather x1, blocking collectives, entering(): pieces = jax.tree.map(lambda part: lax.all_gather(part, axis), value)  39.3 us
  transfers between devices with their start and end apart: 5, of which 3 were waited for; matrix products, arithmetic and copies ran while one was open for 37% of the time, Pallas kernels for 0%

commit v1 on v0

v1 whole, which is shorter than its diff:
```python
import jax
import jax.numpy as jnp
from jax import lax
from jax.experimental import pallas as pl
from jax.experimental.pallas import tpu as pltpu
from jax.sharding import PartitionSpec as P

H = 128
P_SIZE = 64
N = 128
BLOCK = 256
CONV = 4
SLAB = 128
HALO = 8
EPSILON = 1e-05

bf16 = jnp.bfloat16
f32 = jnp.float32


def pieces_of(value):
    high = value.astype(bf16)
    rest = value - high.astype(f32)
    middle = rest.astype(bf16)
    low = (rest - middle.astype(f32)).astype(bf16)
    return high, middle, low


def silu(value):
    return value / (1.0 + jnp.exp(-value))


def convolved(halo, current, taps):
    joined = jnp.concatenate([halo.astype(f32), current.astype(f32)], axis=0)
    height = current.shape[0]
    first = HALO - (CONV - 1)
    summed = taps[0:1] * joined[first : first + height]
    for k in range(1, CONV):
        summed = summed + taps[k : k + 1] * joined[first + k : first + k + height]
    return silu(summed).astype(bf16)


def spread_pair(left, right, rows):
    lane = lax.broadcasted_iota(jnp.int32, (rows, SLAB), 1)
    return jnp.where(
        lane < P_SIZE,
        jnp.broadcast_to(left, (rows, SLAB)),
        jnp.broadcast_to(right, (rows, SLAB)),
    )


def front_kernel(
    x_ref, bc_ref, halo_ref, dt_ref, bias_ref, alog_ref, tapx_ref, tapbc_ref,
    xc_ref, bcv_ref, col_ref, row_ref, send_ref,
):
    heads = dt_ref.shape[0]
    width = x_ref.shape[1]
    raw = dt_ref[...] + bias_ref[...]
    step = jnp.maximum(raw, 0.0) + jnp.log1p(jnp.exp(-jnp.abs(raw)))
    running = -jnp.exp(alog_ref[...]) * step
    lane = lax.broadcasted_iota(jnp.int32, running.shape, 1)
    shift = 1
    while shift < BLOCK:
        moved = pltpu.roll(running, shift, 1)
        running = running + jnp.where(lane >= shift, moved, 0.0)
        shift *= 2
    finish = jnp.exp(running[:, BLOCK - 1 : BLOCK] - running) * step
    row_ref[0:heads] = running
    row_ref[heads : 2 * heads] = step
    columns = jnp.concatenate([running, step, finish, jnp.exp(running)], axis=0).T
    col_ref[...] = columns

    groups = bc_ref.shape[1] // (2 * N)
    turned = []
    for g in range(2 * groups):
        at = slice(g * N, (g + 1) * N)
        here = convolved(halo_ref[:, width + g * N : width + (g + 1) * N], bc_ref[:, at], tapbc_ref[:, at])
        bcv_ref[:, at] = here
        if g % 2 == 0:
            turned.append(here.astype(f32).T.astype(bf16))
    slabs = width // SLAB
    for c in range(slabs):
        at = slice(c * SLAB, (c + 1) * SLAB)
        here = convolved(halo_ref[:, at], x_ref[:, at], tapx_ref[:, at])
        xc_ref[:, at] = here
        h = 2 * c
        weight = spread_pair(
            columns[:, 2 * heads + h : 2 * heads + h + 1],
            columns[:, 2 * heads + h + 1 : 2 * heads + h + 2],
            BLOCK,
        )
        weighted = (here.astype(f32) * weight).astype(bf16)
        fresh = jnp.dot(turned[c // (slabs // groups)], weighted, preferred_element_type=f32)
        decay = spread_pair(
            columns[BLOCK - 1 : BLOCK, 3 * heads + h : 3 * heads + h + 1],
            columns[BLOCK - 1 : BLOCK, 3 * heads + h + 1 : 3 * heads + h + 2],
            8,
        )
        high, middle, low = pieces_of(decay)
        sub = lax.broadcasted_iota(jnp.int32, (8, SLAB), 0)
        lines = jnp.where(
            sub == 0, high.astype(f32), jnp.where(sub == 1, middle.astype(f32), low.astype(f32))
        ).astype(bf16)
        send_ref[2 * c, 0 : N // 2] = fresh[0 : N // 2].astype(bf16)
        send_ref[2 * c + 1, 0 : N // 2] = fresh[N // 2 : N].astype(bf16)
        send_ref[2 * c, N // 2 : N // 2 + 8] = lines
        send_ref[2 * c + 1, N // 2 : N // 2 + 8] = lines


def scan_kernel(got_ref, start_ref):
    count = got_ref.shape[0]
    rows = start_ref.shape[1]

    def advance(j, state):
        start_ref[j] = state.astype(bf16)
        block = got_ref[j].astype(f32)
        decay = block[rows : rows + 1] + block[rows + 1 : rows + 2] + block[rows + 2 : rows + 3]
        return decay * state + block[0:rows]

    lax.fori_loop(0, count, advance, jnp.zeros((rows, SLAB), f32))


def within_kernel(xc_ref, bcv_ref, col_ref, row_ref, skip_ref, out_ref):
    heads = row_ref.shape[0] // 2
    slabs = xc_ref.shape[1] // SLAB
    groups = bcv_ref.shape[1] // (2 * N)
    half = BLOCK // 2
    lane = lax.broadcasted_iota(jnp.int32, (half, SLAB), 1)
    sub = lax.broadcasted_iota(jnp.int32, (half, half), 0)
    across_lane = lax.broadcasted_iota(jnp.int32, (half, half), 1)
    keep = sub >= across_lane
    for g in range(groups):
        b_here = bcv_ref[:, 2 * g * N : (2 * g + 1) * N]
        c_here = bcv_ref[:, (2 * g + 1) * N : (2 * g + 2) * N]
        scores = lax.dot_general(
            c_here, b_here, (((1,), (1,)), ((), ())), preferred_element_type=f32
        )
        for c in range(g * slabs // groups, (g + 1) * slabs // groups):
            at = slice(c * SLAB, (c + 1) * SLAB)
            x_here = xc_ref[:, at]
            parts = []
            for h in (2 * c, 2 * c + 1):
                run_row = row_ref[h : h + 1]
                step_row = row_ref[heads + h : heads + h + 1]
                run_col = jnp.broadcast_to(col_ref[:, h : h + 1], (BLOCK, half))

                def mix(i, j, run_col=run_col, run_row=run_row, step_row=step_row):
                    ri = slice(i * half, (i + 1) * half)
                    rj = slice(j * half, (j + 1) * half)
                    spread = run_col[ri] - run_row[:, rj]
                    if i == j:
                        spread = jnp.where(keep, spread, -jnp.inf)
                    return (scores[ri, rj] * jnp.exp(spread) * step_row[:, rj]).astype(bf16)

                upper = jnp.dot(mix(0, 0), x_here[0:half], preferred_element_type=f32)
                lower = jnp.dot(
                    jnp.concatenate([mix(1, 0), mix(1, 1)], axis=1),
                    x_here,
                    preferred_element_type=f32,
                )
                parts.append((upper, lower))
            skip = skip_ref[:, at]
            for i in range(2):
                ri = slice(i * half, (i + 1) * half)
                out_ref[ri, at] = (
                    jnp.where(lane < P_SIZE, parts[0][i], parts[1][i])
                    + skip * x_here[ri].astype(f32)
                )


def gate_kernel(within_ref, state_ref, bcv_ref, col_ref, z_ref, gain_ref, out_ref, tail_ref):
    heads = col_ref.shape[1] // 4
    slabs = within_ref.shape[1] // SLAB
    groups = bcv_ref.shape[1] // (2 * N)
    squares = jnp.zeros((BLOCK, SLAB), f32)
    for c in range(slabs):
        at = slice(c * SLAB, (c + 1) * SLAB)
        g = c // (slabs // groups)
        c_here = bcv_ref[:, (2 * g + 1) * N : (2 * g + 2) * N]
        across = jnp.dot(c_here, state_ref[c], preferred_element_type=f32)
        h = 3 * heads + 2 * c
        grown = spread_pair(col_ref[:, h : h + 1], col_ref[:, h + 1 : h + 2], BLOCK)
        mixed = within_ref[:, at] + across * grown
        gated = mixed * silu(z_ref[:, at].astype(f32))
        squares = squares + gated * gated
        out_ref[:, at] = (gated * gain_ref[:, at]).astype(bf16)
    line = lax.dot_general(
        jnp.ones((8, SLAB), f32),
        squares,
        (((1,), (1,)), ((), ())),
        preferred_element_type=f32,
        precision=lax.Precision.HIGHEST,
    )
    high, middle, low = pieces_of(line)
    tail_ref[:, 0:BLOCK] = high
    tail_ref[:, BLOCK : 2 * BLOCK] = middle
    tail_ref[:, 2 * BLOCK : 3 * BLOCK] = low
    tail_ref[:, 3 * BLOCK : 4 * BLOCK] = jnp.zeros((8, BLOCK), bf16)


def project_kernel(which_ref, own_ref, other_ref, tail_ref, w_own_ref, w_other_ref, out_ref):
    total = jnp.dot(own_ref[...], w_own_ref[...], preferred_element_type=f32)
    total = total + jnp.dot(other_ref[...], w_other_ref[...], preferred_element_type=f32)
    out_ref[0, 0:BLOCK] = total.astype(bf16)
    out_ref[0, BLOCK : BLOCK + 8] = tail_ref[...]


def finish_kernel(got_ref, out_ref):
    count = got_ref.shape[0]
    total = got_ref[0, 0:BLOCK].astype(f32)
    for k in range(1, count):
        total = total + got_ref[k, 0:BLOCK].astype(f32)
    line = jnp.zeros((8, BLOCK), f32)
    for k in range(count):
        for i in range(3):
            line = line + got_ref[k, BLOCK : BLOCK + 8, i * BLOCK : (i + 1) * BLOCK].astype(f32)
    scale = lax.rsqrt(line / (H * P_SIZE) + EPSILON)
    column = jnp.concatenate([scale] * 16, axis=0).T[:, 0:1]
    out_ref[...] = (total * column).astype(bf16)


def whole(count):
    return [pl.BlockSpec(memory_space=pltpu.VMEM) for _ in range(count)]


def shards(
    x_in, bc_in, z_in, dt_raw, dt_bias, a_log, d_skip, conv_x, conv_bc, norm_gain, out_weight
):
    height, width = x_in.shape
    heads = dt_raw.shape[1]
    nearby = bc_in.shape[1]
    slabs = width // SLAB
    count = lax.axis_size("seq")
    fans = lax.axis_size("head")
    columns = out_weight.shape[1] * count
    rows = width // 2
    core = lax.axis_index("dp")

    w_half = lax.dynamic_slice_in_dim(out_weight, core * rows, rows, 0)
    w_own = lax.all_gather(w_half, "seq", axis=1, tiled=True)
    tail = jnp.concatenate([x_in[height - HALO :], bc_in[height - HALO :]], axis=1)
    halo = lax.ppermute(tail, "seq", [(i, i + 1) for i in range(count - 1)])

    xc, bcv, cols, lines, send = pl.pallas_call(
        front_kernel,
        out_shape=(
            jax.ShapeDtypeStruct((height, width), bf16),
            jax.ShapeDtypeStruct((height, nearby), bf16),
            jax.ShapeDtypeStruct((height, 4 * heads), f32),
            jax.ShapeDtypeStruct((2 * heads, height), f32),
            jax.ShapeDtypeStruct((2 * slabs, N // 2 + 8, SLAB), bf16),
        ),
        in_specs=whole(8),
        out_specs=tuple(whole(5)),
        name="front",
    )(x_in, bc_in, halo, dt_raw.T, dt_bias[:, None], a_log[:, None], conv_x, conv_bc)

    got = lax.all_to_all(send, "seq", 0, 0, tiled=True)
    starts = pl.pallas_call(
        scan_kernel,
        out_shape=jax.ShapeDtypeStruct((count, N // 2, SLAB), bf16),
        in_specs=whole(1),
        out_specs=whole(1)[0],
        name="carry",
    )(got)
    state = lax.all_to_all(starts, "seq", 0, 0, tiled=True).reshape(slabs, N, SLAB)
    w_own, state = lax.optimization_barrier((w_own, state))
    w_other = lax.ppermute(w_own, "dp", [(0, 1), (1, 0)])

    within = pl.pallas_call(
        within_kernel,
        out_shape=jax.ShapeDtypeStruct((height, width), f32),
        in_specs=whole(5),
        out_specs=whole(1)[0],
        name="within",
    )(xc, bcv, cols, lines, jnp.repeat(d_skip, P_SIZE)[None])

    ready, squares = pl.pallas_call(
        gate_kernel,
        out_shape=(
            jax.ShapeDtypeStruct((height, width), bf16),
            jax.ShapeDtypeStruct((8, columns // fans), bf16),
        ),
        in_specs=whole(6),
        out_specs=tuple(whole(2)),
        name="gate",
    )(within, state, bcv, cols, z_in, norm_gain[None])

    share = columns // fans
    partial = pl.pallas_call(
        project_kernel,
        grid_spec=pltpu.PrefetchScalarGridSpec(
            num_scalar_prefetch=1,
            grid=(fans,),
            in_specs=[
                pl.BlockSpec((height, rows), lambda j, s: (0, s[0])),
                pl.BlockSpec((height, rows), lambda j, s: (0, 1 - s[0])),
                pl.BlockSpec((8, share), lambda j, s: (0, 0)),
                pl.BlockSpec((rows, share), lambda j, s: (0, j)),
                pl.BlockSpec((rows, share), lambda j, s: (0, j)),
            ],
            out_specs=pl.BlockSpec((1, height + 8, share), lambda j, s: (j, 0, 0)),
        ),
        out_shape=jax.ShapeDtypeStruct((fans, height + 8, share), bf16),
        name="project",
    )(core.astype(jnp.int32)[None], ready, ready, squares, w_own, w_other)

    swapped = lax.all_to_all(partial, "head", 0, 0, tiled=True)
    return pl.pallas_call(
        finish_kernel,
        out_shape=jax.ShapeDtypeStruct((height, share), bf16),
        in_specs=whole(1),
        out_specs=whole(1)[0],
        name="finish",
    )(swapped)


def solution(mesh):
    placed = (
        P(("dp", "seq"), "head"),
        P(("dp", "seq"), "head"),
        P(("dp", "seq"), "head"),
        P(("dp", "seq"), "head"),
        P("head"),
        P("head"),
        P("head"),
        P(None, "head"),
        P(None, "head"),
        P("head"),
        P("head", "seq"),
    )
    return jax.shard_map(
        shards, mesh=mesh, in_specs=placed, out_specs=P(("dp", "seq"), "head"), check_vma=False
    )
```

time: 519 us -> 191 us (0.37)
  waiting for transfers between devices: 238 us -> 47.2 us
  other arithmetic: 119 us -> 0.01 us
  local copies, waits for them, and re-layouts: 67.4 us -> 7.27 us
  blocking collectives: 47.6 us -> 82.5 us
  Pallas kernels: 0 us -> 30.7 us
  matrix products: 22.3 us -> 0 us
    all_gather x2 -> x1, waiting for transfers between devices: 188 us -> 44.1 us  [shards(): w_own = lax.all_gather(w_half, 'seq', axis=1, tiled=True)]
    select_n x31 -> x0, other arithmetic: 100 us -> none  [lap(): jnp.where(position < mine, new, old)]
    all_to_all x0 -> x3, blocking collectives: none -> 82.5 us  [the longest x1 32 us: shards(): got = lax.all_to_all(send, 'seq', 0, 0, tiled=True)]
    dynamic_slice x62 -> x1, local copies, waits for them, and re-layouts: 59.2 us -> 0.72 us  [shards(): w_half = lax.dynamic_slice_in_dim(out_weight, core * rows, rows, 0)]
    reduce_scatter x1 -> x0, waiting for transfers between devices: 47.3 us -> none  [shards(): lax.psum_scatter(terms, 'head', scatter_dimension=1, tiled=True)]
    all_gather x1 -> x0, blocking collectives: 39.3 us -> none  [entering(): pieces = jax.tree.map(lambda part: lax.all_gather(part, axis), value)]
    pallas_call x0 -> x6, Pallas kernels: none -> 30.7 us  [the longest x1 9.84 us: shards(): pl.pallas_call(project_kernel, grid_spec=pltpu.PrefetchScalarGridSpec(num...]
    dot_general x5 -> x0, matrix products: 22.3 us -> none  [the longest x1 10.3 us: shards(): jnp.dot(normed, lax.all_gather(out_weight, 'seq', axis=1, tiled=True), pr...]
  transfers between devices with their start and end apart: 5 -> 3, of which waited for: 3 -> 2; matrix products, arithmetic and copies ran while one was open for 37% -> 3% of each run, Pallas kernels for 0% -> 10%
where the time goes in v1:
time: 191 us; the launch traced here: 190 us
  blocking collectives  82.5 us (43%)
  waiting for transfers between devices  47.2 us (25%)
  Pallas kernels  30.7 us (16%)
  between operations  13.4 us (7%)
  starting transfers between devices  8.66 us (5%)
  local copies, waits for them, and re-layouts  7.27 us (4%)
    all_gather x1, waiting for transfers between devices, shards(): w_own = lax.all_gather(w_half, 'seq', axis=1, tiled=True)  44.1 us
    all_to_all x1, blocking collectives, shards(): got = lax.all_to_all(send, 'seq', 0, 0, tiled=True)  32 us
    all_to_all x1, blocking collectives, shards(): swapped = lax.all_to_all(partial, 'head', 0, 0, tiled=True)  30.9 us
    all_to_all x1, blocking collectives, shards(): lax.all_to_all(starts, 'seq', 0, 0, tiled=True).reshape(slabs, N, SLAB)  19.6 us
    pallas_call x1, Pallas kernels, shards(): pl.pallas_call(project_kernel, grid_spec=pltpu.PrefetchScalarGridSpec(num...  9.84 us
    pallas_call x1, Pallas kernels, shards(): pl.pallas_call(front_kernel, out_shape=(jax.ShapeDtypeStruct((height, wid...  6.67 us
    pallas_call x1, Pallas kernels, shards(): pl.pallas_call(within_kernel, out_shape=jax.ShapeDtypeStruct((height, wid...  4.75 us
    ppermute x1, starting transfers between devices, shards(): w_other = lax.ppermute(w_own, 'dp', [(0, 1), (1, 0)])  4.65 us
  transfers between devices with their start and end apart: 3, of which 2 were waited for; matrix products, arithmetic and copies ran while one was open for 3% of the time, Pallas kernels for 10%

profile of v1, /device:TPU:1, one launch (start us, length us, event | category | flops | bytes accessed | tf_op | source)
XLA Modules:
  0.0 189.8 jit_solution(16006765776160216894)
XLA Ops:
  6.5 1.0 copy-done
  7.6 0.7 constant_dynamic-slice_fusion
  8.3 0.0 all-gather.2.cloned.1.call-update
  8.3 0.7 slice.7
  9.0 0.8 slice.6
  9.8 4.0 %collective-permute-start = (bf16[8,2560]{1,0:T(8,128)(2,1)S(1)}, bf16[8,2560]{1,0:T(8,128)(2,1)S(1)}, u32[]{:S(2)}, u32[]{:S(2)}) collective-permute-start(bf16[8,2560]{1,0:T(8,128)(2,1)S(1)} %pad_maximum_fusion), channel_id=1, source_target_pairs={{0,8},{8,16},{16,24},{24,32},{32,40},{40,48},{48,56},{56,64},{64,7... | collective-permute-start | bytes 122888 | tf_op jit(solution)/shard_map/ppermute | solution.py:242
  13.8 1.3 copy.12.bias_ref
  15.1 1.3 copy.13.alog_ref
  16.5 0.0 collective-permute-done.halo_ref
  16.5 0.6 copy-done.1
  17.1 6.7 %front.1 = (bf16[256,2048]{1,0:T(8,128)(2,1)}, bf16[256,512]{1,0:T(8,128)(2,1)}, f32[256,128]{1,0:T(8,128)}, f32[64,256]{1,0:T(8,128)}, bf16[32,72,128]{2,1,0:T(8,128)(2,1)}) custom-call(bf16[256,2048]{1,0:T(8,128)(2,1)} %x_ref.1, bf16[256,512]{1,0:T(8,128)(2,1)} %bc_ref.1, bf16[8,2560]{1,0:T(8,128)(2,1)} %copy-done.1, f32[32,256]{1,0:T(8,128)} %bitcast.7, ...), custom_call_target="tpu_custom_call" | custom-call | tf_op jit(solution)/shard_map/front/pallas_call | solution.py:244
  23.8 32.0 %all_to_all.15.got_ref = bf16[32,72,128]{2,1,0:T(8,128)(2,1)} all-to-all(bf16[32,72,128]{2,1,0:T(8,128)(2,1)} %get-tuple-element.18), channel_id=1, replica_groups=mesh['seq'=32,'head'=4,'dp'=2] {'seq'}, dimensions={0} | all-to-all | bytes 1179648 | tf_op jit(solution)/shard_map/all_to_all | solution.py:258
  55.8 2.2 %carry.1 = bf16[32,64,128]{2,1,0:T(8,128)(2,1)} custom-call(bf16[32,72,128]{2,1,0:T(8,128)(2,1)} %all_to_all.15.got_ref), custom_call_target="tpu_custom_call" | custom-call | tf_op jit(solution)/shard_map/carry/pallas_call | solution.py:259
  58.0 19.6 %all_to_all.16 = bf16[32,64,128]{2,1,0:T(8,128)(2,1)} all-to-all(bf16[32,64,128]{2,1,0:T(8,128)(2,1)} %carry.1), channel_id=1, replica_groups=mesh['seq'=32,'head'=4,'dp'=2] {'seq'}, dimensions={0} | all-to-all | bytes 1048576 | tf_op jit(solution)/shard_map/all_to_all | solution.py:266
  77.5 44.1 %all-gather.2.cloned.1.call-done.w_own_ref = bf16[1024,4096]{1,0:T(8,128)(2,1)} async-done(((bf16[1024,128]{1,0:T(8,128)(2,1)}), bf16[1024,4096]{1,0:T(8,128)(2,1)}) %all-gather.2.cloned.1.call-update) | async-done | bytes 8388624 | tf_op jit(solution)/shard_map/all_gather | solution.py:240
  121.6 4.7 %collective-permute-start.1 = (bf16[1024,4096]{1,0:T(8,128)(2,1)}, bf16[1024,4096]{1,0:T(8,128)(2,1)}, u32[]{:S(2)}, u32[]{:S(2)}) collective-permute-start(bf16[1024,4096]{1,0:T(8,128)(2,1)} %all-gather.2.cloned.1.call-done.w_own_ref), channel_id=1, source_target_pairs={{0,1},{1,0},{2,3},{3,2},{4,5},{5,4},{6,7},{7,6},{8,9},{9,8},{10,11... | collective-permute-start | bytes 25165832 | tf_op jit(solution)/shard_map/ppermute | solution.py:268
  126.3 0.1 broadcast_in_dim.18
  126.3 0.7 broadcast_in_dim_reshape.3.skip_ref
  127.0 4.8 %within.1.within_ref = f32[256,2048]{1,0:T(8,128)} custom-call(bf16[256,2048]{1,0:T(8,128)(2,1)} %get-tuple-element.14.xc_ref, bf16[256,512]{1,0:T(8,128)(2,1)} %get-tuple-element.15.bcv_ref, f32[256,128]{1,0:T(8,128)} %get-tuple-element.16.col_ref, f32[64,256]{1,0:T(8,128)} %get-tuple-element.17.row_ref, f32[1,2048]{1,0:T(1,128)} %broadcast_in_dim_reshape.3.skip_ref), custom_call_target="tpu_custom_call" | custom-call | tf_op jit(solution)/shard_map/within/pallas_call | solution.py:270
  131.8 4.5 %gate.1 = (bf16[256,2048]{1,0:T(8,128)(2,1)}, bf16[8,1024]{1,0:T(8,128)(2,1)}) custom-call(f32[256,2048]{1,0:T(8,128)} %within.1.within_ref, bf16[16,128,128]{2,1,0:T(8,128)(2,1)} %bitcast.6, bf16[256,512]{1,0:T(8,128)(2,1)} %get-tuple-element.15.bcv_ref, f32[256,128]{1,0:T(8,128)} %get-tuple-element.16.col_ref, bf16[256,2048]{1,0:T(8,128)(2,1)} %z_ref.1, ...), custom_call_target="tpu_custom_call" | custom-call | tf_op jit(solution)/shard_map/gate/pallas_call | solution.py:278
  136.2 3.1 %collective-permute-done.1.w_other_ref = bf16[1024,4096]{1,0:T(8,128)(2,1)} collective-permute-done((bf16[1024,4096]{1,0:T(8,128)(2,1)}, bf16[1024,4096]{1,0:T(8,128)(2,1)}, u32[]{:S(2)}, u32[]{:S(2)}) %collective-permute-start.1) | collective-permute-done | bytes 8388640 | tf_op jit(solution)/shard_map/ppermute | solution.py:268
  139.4 9.8 %project.1 = bf16[4,264,1024]{2,1,0:T(8,128)(2,1)} custom-call(s32[1]{0:T(128)} %bitcast.which_ref, bf16[256,2048]{1,0:T(8,128)(2,1)} %get-tuple-element.20.own_ref.other_ref, bf16[256,2048]{1,0:T(8,128)(2,1)} %get-tuple-element.20.own_ref.other_ref, bf16[8,1024]{1,0:T(8,128)(2,1)} %get-tuple-element.21.tail_ref, ...), custom_call_target="tpu_custom_call" | custom-call | tf_op jit(solution)/shard_map/project/pallas_call | solution.py:290
  149.2 30.9 %all_to_all.17.got_ref = bf16[4,264,1024]{2,1,0:T(8,128)(2,1)} all-to-all(bf16[4,264,1024]{2,1,0:T(8,128)(2,1)} %project.1), channel_id=1, replica_groups=mesh['seq'=32,'head'=4,'dp'=2] {'head'}, dimensions={0} | all-to-all | bytes 4325376 | tf_op jit(solution)/shard_map/all_to_all | solution.py:308
  180.1 2.8 %finish.1 = bf16[256,1024]{1,0:T(8,128)(2,1)} custom-call(bf16[4,264,1024]{2,1,0:T(8,128)(2,1)} %all_to_all.17.got_ref), custom_call_target="tpu_custom_call" | custom-call | tf_op jit(solution)/shard_map/finish/pallas_call | solution.py:309
  (6 shorter events, 0.0 us)
Async XLA Ops:
  6.5 1.0 copy-start
  6.5 115.1 %all-gather.2.cloned.1.call-start = ((), (), s32[]{:S(2)}) async-start(), calls=%async_computation.3 | async-start | bytes 8650752 | tf_op jit(solution)/shard_map/all_gather | solution.py:240
  9.8 6.7 %collective-permute-start = (bf16[8,2560]{1,0:T(8,128)(2,1)S(1)}, bf16[8,2560]{1,0:T(8,128)(2,1)S(1)}, u32[]{:S(2)}, u32[]{:S(2)}) collective-permute-start(bf16[8,2560]{1,0:T(8,128)(2,1)S(1)} %pad_maximum_fusion), channel_id=1, source_target_pairs={{0,8},{8,16},{16,24},{24,32},{32,40},{40,48},{48,56},{56,64},{64,7... | collective-permute-start | bytes 122888 | tf_op jit(solution)/shard_map/ppermute | solution.py:242
  16.5 0.6 copy-start.1
  17.1 109.2 %copy-start.2 = (f32[32]{0:T(128)S(1)}, f32[32]{0:T(128)}, u32[]{:S(2)}) copy-start(f32[32]{0:T(128)} %param.17) | copy-start | bytes 388
  121.6 17.8 %collective-permute-start.1 = (bf16[1024,4096]{1,0:T(8,128)(2,1)}, bf16[1024,4096]{1,0:T(8,128)(2,1)}, u32[]{:S(2)}, u32[]{:S(2)}) collective-permute-start(bf16[1024,4096]{1,0:T(8,128)(2,1)} %all-gather.2.cloned.1.call-done.w_own_ref), channel_id=1, source_target_pairs={{0,1},{1,0},{2,3},{3,2},{4,5},{5,4},{6,7},{7,6},{8,9},{9,8},{10,11... | collective-permute-start | bytes 25165832 | tf_op jit(solution)/shard_map/ppermute | solution.py:268
Sparse Core Ops, SparseCore 0:
  9.8 111.7 all-gather.1

commit v2 on v1

--- a/solution.py
+++ b/solution.py
@@ -12,6 +12,7 @@
 CONV = 4
 SLAB = 128
 HALO = 8
+TAIL = 8
 EPSILON = 1e-05
 
 bf16 = jnp.bfloat16
@@ -55,9 +56,17 @@
 ):
     heads = dt_ref.shape[0]
     width = x_ref.shape[1]
-    raw = dt_ref[...] + bias_ref[...]
+    diagonal = lax.broadcasted_iota(jnp.int32, (heads, heads), 0) == lax.broadcasted_iota(
+        jnp.int32, (heads, heads), 1
+    )
+
+    def stood(line):
+        square = jnp.broadcast_to(line, (heads, heads))
+        return jnp.sum(jnp.where(diagonal, square, 0.0), axis=1, keepdims=True)
+
+    raw = dt_ref[...] + stood(bias_ref[...])
     step = jnp.maximum(raw, 0.0) + jnp.log1p(jnp.exp(-jnp.abs(raw)))
-    running = -jnp.exp(alog_ref[...]) * step
+    running = -jnp.exp(stood(alog_ref[...])) * step
     lane = lax.broadcasted_iota(jnp.int32, running.shape, 1)
     shift = 1
     while shift < BLOCK:
@@ -168,7 +177,7 @@
                 )
 
 
-def gate_kernel(within_ref, state_ref, bcv_ref, col_ref, z_ref, gain_ref, out_ref, tail_ref):
+def gate_kernel(within_ref, state_ref, bcv_ref, col_ref, z_ref, gain_ref, out_ref):
     heads = col_ref.shape[1] // 4
     slabs = within_ref.shape[1] // SLAB
     groups = bcv_ref.shape[1] // (2 * N)
@@ -183,40 +192,63 @@
         mixed = within_ref[:, at] + across * grown
         gated = mixed * silu(z_ref[:, at].astype(f32))
         squares = squares + gated * gated
-        out_ref[:, at] = (gated * gain_ref[:, at]).astype(bf16)
+        out_ref[0:BLOCK, at] = (gated * gain_ref[:, at]).astype(bf16)
     line = lax.dot_general(
-        jnp.ones((8, SLAB), f32),
+        jnp.ones((TAIL, SLAB), f32),
         squares,
         (((1,), (1,)), ((), ())),
         preferred_element_type=f32,
         precision=lax.Precision.HIGHEST,
     )
-    high, middle, low = pieces_of(line)
-    tail_ref[:, 0:BLOCK] = high
-    tail_ref[:, BLOCK : 2 * BLOCK] = middle
-    tail_ref[:, 2 * BLOCK : 3 * BLOCK] = low
-    tail_ref[:, 3 * BLOCK : 4 * BLOCK] = jnp.zeros((8, BLOCK), bf16)
-
-
-def project_kernel(which_ref, own_ref, other_ref, tail_ref, w_own_ref, w_other_ref, out_ref):
-    total = jnp.dot(own_ref[...], w_own_ref[...], preferred_element_type=f32)
-    total = total + jnp.dot(other_ref[...], w_other_ref[...], preferred_element_type=f32)
-    out_ref[0, 0:BLOCK] = total.astype(bf16)
-    out_ref[0, BLOCK : BLOCK + 8] = tail_ref[...]
+    end = slice(BLOCK, BLOCK + TAIL)
+    out_ref[end, 2 * BLOCK :] = jnp.zeros((TAIL, within_ref.shape[1] - 2 * BLOCK), bf16)
+    for i, piece in enumerate(pieces_of(line)[0:2]):
+        out_ref[end, i * BLOCK : (i + 1) * BLOCK] = piece
+
+
+def turn_kernel(core_ref, w_ref, out_ref, turned_ref):
+    turned_ref[...] = w_ref[...].astype(f32).T
+    rows = out_ref.shape[0]
+    first = pl.multiple_of(core_ref[0] * rows, rows)
+    out_ref[...] = turned_ref[pl.ds(first, rows)].astype(bf16)
+
+
+def against(left, right):
+    return lax.dot_general(left, right, (((1,), (1,)), ((), ())), preferred_element_type=f32)
+
+
+def project_kernel(core_ref, own_ref, other_ref, w_ref, out_ref):
+    core = core_ref[0]
+    end = slice(BLOCK, BLOCK + TAIL)
+    for seat, ref in ((core, own_ref), (1 - core, other_ref)):
+        out_ref[seat, 0:BLOCK] = against(ref[0:BLOCK], w_ref[...]).astype(bf16)
+        out_ref[seat, end] = ref[end, 0 : 2 * BLOCK]
 
 
 def finish_kernel(got_ref, out_ref):
-    count = got_ref.shape[0]
-    total = got_ref[0, 0:BLOCK].astype(f32)
-    for k in range(1, count):
-        total = total + got_ref[k, 0:BLOCK].astype(f32)
-    line = jnp.zeros((8, BLOCK), f32)
-    for k in range(count):
-        for i in range(3):
-            line = line + got_ref[k, BLOCK : BLOCK + 8, i * BLOCK : (i + 1) * BLOCK].astype(f32)
+    sources = got_ref.shape[0]
+    end = slice(BLOCK, BLOCK + TAIL)
+    line = jnp.zeros((TAIL, BLOCK), f32)
+    for k in range(0, sources, 2):
+        for i in range(2):
+            line = line + got_ref[k, end, i * BLOCK : (i + 1) * BLOCK].astype(f32)
     scale = lax.rsqrt(line / (H * P_SIZE) + EPSILON)
-    column = jnp.concatenate([scale] * 16, axis=0).T[:, 0:1]
-    out_ref[...] = (total * column).astype(bf16)
+    column = jnp.concatenate([scale] * (SLAB // TAIL), axis=0).T[:, 0:1]
+    scale = jnp.broadcast_to(column, (BLOCK, SLAB))
+    lane = lax.broadcasted_iota(jnp.int32, (BLOCK, SLAB), 1)
+    half = SLAB // 2
+    for m in range(got_ref.shape[2] // SLAB):
+        at = slice(m * SLAB, (m + 1) * SLAB)
+        sums = []
+        for d in range(2):
+            total = got_ref[d, 0:BLOCK, at].astype(f32)
+            for k in range(d + 2, sources, 2):
+                total = total + got_ref[k, 0:BLOCK, at].astype(f32)
+            sums.append(total * scale)
+        first = jnp.where(lane < half, sums[0], pltpu.roll(sums[1], half, 1))
+        second = jnp.where(lane < half, pltpu.roll(sums[0], half, 1), sums[1])
+        out_ref[:, 2 * m * SLAB : (2 * m + 1) * SLAB] = first.astype(bf16)
+        out_ref[:, (2 * m + 1) * SLAB : (2 * m + 2) * SLAB] = second.astype(bf16)
 
 
 def whole(count):
@@ -232,14 +264,22 @@
     slabs = width // SLAB
     count = lax.axis_size("seq")
     fans = lax.axis_size("head")
-    columns = out_weight.shape[1] * count
-    rows = width // 2
     core = lax.axis_index("dp")
 
-    w_half = lax.dynamic_slice_in_dim(out_weight, core * rows, rows, 0)
-    w_own = lax.all_gather(w_half, "seq", axis=1, tiled=True)
     tail = jnp.concatenate([x_in[height - HALO :], bc_in[height - HALO :]], axis=1)
     halo = lax.ppermute(tail, "seq", [(i, i + 1) for i in range(count - 1)])
+
+    seat = core.astype(jnp.int32)[None]
+    piece_rows = out_weight.shape[1] // 2
+    piece = pl.pallas_call(
+        turn_kernel,
+        out_shape=jax.ShapeDtypeStruct((piece_rows, width), bf16),
+        in_specs=[pl.BlockSpec(memory_space=pltpu.SMEM)] + whole(1),
+        out_specs=whole(1)[0],
+        scratch_shapes=[pltpu.VMEM((2 * piece_rows, width), f32)],
+        name="turn",
+    )(seat, out_weight)
+    weights = lax.all_gather(piece, "seq", axis=0, tiled=True)
 
     xc, bcv, cols, lines, send = pl.pallas_call(
         front_kernel,
@@ -253,7 +293,7 @@
         in_specs=whole(8),
         out_specs=tuple(whole(5)),
         name="front",
-    )(x_in, bc_in, halo, dt_raw.T, dt_bias[:, None], a_log[:, None], conv_x, conv_bc)
+    )(x_in, bc_in, halo, dt_raw.T, dt_bias[None], a_log[None], conv_x, conv_bc)
 
     got = lax.all_to_all(send, "seq", 0, 0, tiled=True)
     starts = pl.pallas_call(
@@ -264,8 +304,6 @@
         name="carry",
     )(got)
     state = lax.all_to_all(starts, "seq", 0, 0, tiled=True).reshape(slabs, N, SLAB)
-    w_own, state = lax.optimization_barrier((w_own, state))
-    w_other = lax.ppermute(w_own, "dp", [(0, 1), (1, 0)])
 
     within = pl.pallas_call(
         within_kernel,
@@ -275,40 +313,36 @@
         name="within",
     )(xc, bcv, cols, lines, jnp.repeat(d_skip, P_SIZE)[None])
 
-    ready, squares = pl.pallas_call(
+    ready = pl.pallas_call(
         gate_kernel,
-        out_shape=(
-            jax.ShapeDtypeStruct((height, width), bf16),
-            jax.ShapeDtypeStruct((8, columns // fans), bf16),
-        ),
+        out_shape=jax.ShapeDtypeStruct((height + TAIL, width), bf16),
         in_specs=whole(6),
-        out_specs=tuple(whole(2)),
+        out_specs=whole(1)[0],
         name="gate",
     )(within, state, bcv, cols, z_in, norm_gain[None])
 
-    share = columns // fans
+    other = lax.ppermute(ready, "dp", [(0, 1), (1, 0)])
+    share = piece_rows * count // fans
     partial = pl.pallas_call(
         project_kernel,
         grid_spec=pltpu.PrefetchScalarGridSpec(
             num_scalar_prefetch=1,
             grid=(fans,),
             in_specs=[
-                pl.BlockSpec((height, rows), lambda j, s: (0, s[0])),
-                pl.BlockSpec((height, rows), lambda j, s: (0, 1 - s[0])),
-                pl.BlockSpec((8, share), lambda j, s: (0, 0)),
-                pl.BlockSpec((rows, share), lambda j, s: (0, j)),
-                pl.BlockSpec((rows, share), lambda j, s: (0, j)),
+                pl.BlockSpec((height + TAIL, width), lambda j, s: (0, 0)),
+                pl.BlockSpec((height + TAIL, width), lambda j, s: (0, 0)),
+                pl.BlockSpec((share, width), lambda j, s: (j, 0)),
             ],
-            out_specs=pl.BlockSpec((1, height + 8, share), lambda j, s: (j, 0, 0)),
+            out_specs=pl.BlockSpec((2, height + TAIL, share), lambda j, s: (j, 0, 0)),
         ),
-        out_shape=jax.ShapeDtypeStruct((fans, height + 8, share), bf16),
+        out_shape=jax.ShapeDtypeStruct((2 * fans, height + TAIL, share), bf16),
         name="project",
-    )(core.astype(jnp.int32)[None], ready, ready, squares, w_own, w_other)
-
-    swapped = lax.all_to_all(partial, "head", 0, 0, tiled=True)
+    )(seat, ready, other, weights)
+
+    swapped = lax.all_to_all(partial, ("head", "dp"), 0, 0, tiled=True)
     return pl.pallas_call(
         finish_kernel,
-        out_shape=jax.ShapeDtypeStruct((height, share), bf16),
+        out_shape=jax.ShapeDtypeStruct((height, 2 * share), bf16),
         in_specs=whole(1),
         out_specs=whole(1)[0],
         name="finish",

time: 191 us -> 172 us (0.901)
  blocking collectives: 82.5 us -> 67.1 us
  waiting for transfers between devices: 47.2 us -> 39.1 us
  starting transfers between devices: 8.66 us -> 16.2 us
  local copies, waits for them, and re-layouts: 7.27 us -> 3.62 us
    all_gather x1, waiting for transfers between devices: 44.1 us -> 23.4 us  [shards(): weights = lax.all_gather(piece, 'seq', axis=0, tiled=True)]
    all_to_all x2 -> x1, blocking collectives: 50.5 us -> 32.8 us  [shards(): swapped = lax.all_to_all(partial, ('head', 'dp'), 0, 0, tiled=True)]
    all_to_all x0 -> x1, waiting for transfers between devices: none -> 12 us  [shards(): lax.all_to_all(starts, 'seq', 0, 0, tiled=True).reshape(slabs, N, SLAB)]
    all_to_all x0 -> x1, starting transfers between devices: none -> 6.44 us  [shards(): lax.all_to_all(starts, 'seq', 0, 0, tiled=True).reshape(slabs, N, SLAB)]
    broadcast_in_dim x2 -> x0, local copies, waits for them, and re-layouts: 2.67 us -> none  [the longest x1 1.34 us: shards(): a_log[:, None]]
    pallas_call x2 -> x3, Pallas kernels: 7.25 us -> 9.71 us  [the longest x1 4.8 us: shards(): pl.pallas_call(gate_kernel, out_shape=jax.ShapeDtypeStruct((height + TAIL...]
    all_to_all x1, blocking collectives: 32 us -> 34.4 us  [shards(): got = lax.all_to_all(send, 'seq', 0, 0, tiled=True)]
  transfers between devices with their start and end apart: 3 -> 4, of which waited for: 2 -> 4; matrix products, arithmetic and copies ran while one was open for 3% -> 1% of each run, Pallas kernels for 10% -> 11%
where the time goes in v2:
time: 172 us
  blocking collectives  67.1 us (39%)
  waiting for transfers between devices  39.1 us (23%)
  Pallas kernels  32.1 us (19%)
  starting transfers between devices  16.2 us (9%)
  between operations  13.4 us (8%)
  local copies, waits for them, and re-layouts  3.62 us (2%)
    all_to_all x1, blocking collectives, shards(): got = lax.all_to_all(send, 'seq', 0, 0, tiled=True)  34.4 us
    all_to_all x1, blocking collectives, shards(): swapped = lax.all_to_all(partial, ('head', 'dp'), 0, 0, tiled=True)  32.8 us
    all_gather x1, waiting for transfers between devices, shards(): weights = lax.all_gather(piece, 'seq', axis=0, tiled=True)  23.4 us
    all_to_all x1, waiting for transfers between devices, shards(): lax.all_to_all(starts, 'seq', 0, 0, tiled=True).reshape(slabs, N, SLAB)  12 us
    pallas_call x1, Pallas kernels, shards(): pl.pallas_call(project_kernel, grid_spec=pltpu.PrefetchScalarGridSpec(num...  8.8 us
    pallas_call x1, Pallas kernels, shards(): pl.pallas_call(front_kernel, out_shape=(jax.ShapeDtypeStruct((height, wid...  6.69 us
    all_to_all x1, starting transfers between devices, shards(): lax.all_to_all(starts, 'seq', 0, 0, tiled=True).reshape(slabs, N, SLAB)  6.44 us
    ppermute x1, starting transfers between devices, shards(): other = lax.ppermute(ready, 'dp', [(0, 1), (1, 0)])  5.72 us
  transfers between devices with their start and end apart: 4, of which 4 were waited for; matrix products, arithmetic and copies ran while one was open for 1% of the time, Pallas kernels for 11%

profile of v2, /device:TPU:1, one launch (start us, length us, event | category | flops | bytes accessed | tf_op | source)
XLA Modules:
  0.0 171.6 jit_solution(8646514370326109957)
XLA Ops:
  6.5 0.0 all-gather.2.cloned.1.call-start
  6.5 2.0 %turn.1 = bf16[64,2048]{1,0:T(8,128)(2,1)} custom-call(s32[1]{0:T(128)} %bitcast.core_ref, bf16[2048,128]{1,0:T(8,128)(2,1)} %w_ref.1), custom_call_target="tpu_custom_call" | custom-call | tf_op jit(solution)/shard_map/turn/pallas_call | solution.py:274
  8.5 0.0 all-gather.2.cloned.1.call-update
  8.6 0.7 slice.7
  9.3 0.8 slice.6
  10.0 4.0 %collective-permute-start = (bf16[8,2560]{1,0:T(8,128)(2,1)S(1)}, bf16[8,2560]{1,0:T(8,128)(2,1)S(1)}, u32[]{:S(2)}, u32[]{:S(2)}) collective-permute-start(bf16[8,2560]{1,0:T(8,128)(2,1)S(1)} %pad_maximum_fusion), channel_id=1, source_target_pairs={{0,8},{8,16},{16,24},{24,32},{32,40},{40,48},{48,56},{56,64},{64,7... | collective-permute-start | bytes 122888 | tf_op jit(solution)/shard_map/ppermute | solution.py:270
  14.0 1.1 collective-permute-done.halo_ref
  15.1 0.6 copy-done.2
  15.7 6.7 %front.1 = (bf16[256,2048]{1,0:T(8,128)(2,1)}, bf16[256,512]{1,0:T(8,128)(2,1)}, f32[256,128]{1,0:T(8,128)}, f32[64,256]{1,0:T(8,128)}, bf16[32,72,128]{2,1,0:T(8,128)(2,1)}) custom-call(bf16[256,2048]{1,0:T(8,128)(2,1)} %x_ref.1, bf16[256,512]{1,0:T(8,128)(2,1)} %bc_ref.1, bf16[8,2560]{1,0:T(8,128)(2,1)} %copy-done.2, f32[32,256]{1,0:T(8,128)} %bitcast.7, ...), custom_call_target="tpu_custom_call" | custom-call | tf_op jit(solution)/shard_map/front/pallas_call | solution.py:284
  22.4 34.4 %all_to_all.15.got_ref = bf16[32,72,128]{2,1,0:T(8,128)(2,1)} all-to-all(bf16[32,72,128]{2,1,0:T(8,128)(2,1)} %get-tuple-element.14), channel_id=1, replica_groups=mesh['seq'=32,'head'=4,'dp'=2] {'seq'}, dimensions={0} | all-to-all | bytes 1179648 | tf_op jit(solution)/shard_map/all_to_all | solution.py:298
  56.8 2.2 %carry.1 = bf16[32,64,128]{2,1,0:T(8,128)(2,1)} custom-call(bf16[32,72,128]{2,1,0:T(8,128)(2,1)} %all_to_all.15.got_ref), custom_call_target="tpu_custom_call" | custom-call | tf_op jit(solution)/shard_map/carry/pallas_call | solution.py:299
  59.0 6.4 %all-to-all-start.1 = ((bf16[32,64,128]{2,1,0:T(8,128)(2,1)}), bf16[32,64,128]{2,1,0:T(8,128)(2,1)S(1)}, u32[]{:S(2)}, u32[]{:S(2)}) async-start(bf16[32,64,128]{2,1,0:T(8,128)(2,1)} %carry.1), calls=%async_computation.1 | async-start | bytes 1048576 | tf_op jit(solution)/shard_map/all_to_all | solution.py:306
  65.5 0.1 broadcast_in_dim.18
  65.5 0.7 broadcast_in_dim_reshape.3.skip_ref
  66.2 4.8 %within.1.within_ref = f32[256,2048]{1,0:T(8,128)} custom-call(bf16[256,2048]{1,0:T(8,128)(2,1)} %get-tuple-element.10.xc_ref, bf16[256,512]{1,0:T(8,128)(2,1)} %get-tuple-element.11.bcv_ref, f32[256,128]{1,0:T(8,128)} %get-tuple-element.12.col_ref, f32[64,256]{1,0:T(8,128)} %get-tuple-element.13.row_ref, f32[1,2048]{1,0:T(1,128)} %broadcast_in_dim_reshape.3.skip_ref), custom_call_target="tpu_custom_call" | custom-call | tf_op jit(solution)/shard_map/within/pallas_call | solution.py:308
  71.0 12.0 %all-to-all-done.1 = bf16[32,64,128]{2,1,0:T(8,128)(2,1)S(1)} async-done(((bf16[32,64,128]{2,1,0:T(8,128)(2,1)}), bf16[32,64,128]{2,1,0:T(8,128)(2,1)S(1)}, u32[]{:S(2)}, u32[]{:S(2)}) %all-to-all-start.1) | async-done | bytes 524320 | tf_op jit(solution)/shard_map/all_to_all | solution.py:306
  83.0 0.8 copy-done
  83.8 4.8 %gate.1.own_ref = bf16[264,2048]{1,0:T(8,128)(2,1)} custom-call(f32[256,2048]{1,0:T(8,128)} %within.1.within_ref, bf16[16,128,128]{2,1,0:T(8,128)(2,1)} %bitcast.6, bf16[256,512]{1,0:T(8,128)(2,1)} %get-tuple-element.11.bcv_ref, f32[256,128]{1,0:T(8,128)} %get-tuple-element.12.col_ref, bf16[256,2048]{1,0:T(8,128)(2,1)} %z_ref.1, f32[1,2048]{1,0:T(1,128)} %bitcast.8), custom_call_target="tpu_custom_call" | custom-call | tf_op jit(solution)/shard_map/gate/pallas_call | solution.py:316
  88.6 5.7 %collective-permute-start.1 = (bf16[264,2048]{1,0:T(8,128)(2,1)}, bf16[264,2048]{1,0:T(8,128)(2,1)S(1)}, u32[]{:S(2)}, u32[]{:S(2)}) collective-permute-start(bf16[264,2048]{1,0:T(8,128)(2,1)} %gate.1.own_ref), channel_id=1, source_target_pairs={{0,1},{1,0},{2,3},{3,2},{4,5},{5,4},{6,7},{7,6},{8,9},{9,8},{10,11... | collective-permute-start | bytes 3244040 | tf_op jit(solution)/shard_map/ppermute | solution.py:324
  94.3 2.5 %collective-permute-done.1.other_ref = bf16[264,2048]{1,0:T(8,128)(2,1)S(1)} collective-permute-done((bf16[264,2048]{1,0:T(8,128)(2,1)}, bf16[264,2048]{1,0:T(8,128)(2,1)S(1)}, u32[]{:S(2)}, u32[]{:S(2)}) %collective-permute-start.1) | collective-permute-done | bytes 1081376 | tf_op jit(solution)/shard_map/ppermute | solution.py:324
  96.9 23.4 %all-gather.2.cloned.1.call-done.w_ref = bf16[2048,2048]{1,0:T(8,128)(2,1)} async-done(((bf16[64,2048]{1,0:T(8,128)(2,1)}), bf16[2048,2048]{1,0:T(8,128)(2,1)}) %all-gather.2.cloned.1.call-update) | async-done | bytes 8388624 | tf_op jit(solution)/shard_map/all_gather | solution.py:282
  120.3 8.8 %project.1 = bf16[8,264,512]{2,1,0:T(8,128)(2,1)} custom-call(s32[1]{0:T(128)} %bitcast.core_ref, bf16[264,2048]{1,0:T(8,128)(2,1)} %gate.1.own_ref, bf16[264,2048]{1,0:T(8,128)(2,1)} %copy-done.1, bf16[2048,2048]{1,0:T(8,128)(2,1)} %all-gather.2.cloned.1.call-done.w_ref), custom_call_target="tpu_custom_call" | custom-call | tf_op jit(solution)/shard_map/project/pallas_call | solution.py:326
  129.1 32.8 %all_to_all.16.got_ref = bf16[8,264,512]{2,1,0:T(8,128)(2,1)} all-to-all(bf16[8,264,512]{2,1,0:T(8,128)(2,1)} %project.1), channel_id=1, replica_groups=mesh['seq'=32,'head'=4,'dp'=2] {'head','dp'}, dimensions={0} | all-to-all | bytes 4325376 | tf_op jit(solution)/shard_map/all_to_all | solution.py:342
  161.9 2.9 %finish.1 = bf16[256,1024]{1,0:T(8,128)(2,1)} custom-call(bf16[8,264,512]{2,1,0:T(8,128)(2,1)} %all_to_all.16.got_ref), custom_call_target="tpu_custom_call" | custom-call | tf_op jit(solution)/shard_map/finish/pallas_call | solution.py:343
  (7 shorter events, 0.0 us)
Async XLA Ops:
  6.5 113.8 %all-gather.2.cloned.1.call-start = ((), (), s32[]{:S(2)}) async-start(), calls=%async_computation.3 | async-start | bytes 8650752 | tf_op jit(solution)/shard_map/all_gather | solution.py:282
  10.0 5.1 %collective-permute-start = (bf16[8,2560]{1,0:T(8,128)(2,1)S(1)}, bf16[8,2560]{1,0:T(8,128)(2,1)S(1)}, u32[]{:S(2)}, u32[]{:S(2)}) collective-permute-start(bf16[8,2560]{1,0:T(8,128)(2,1)S(1)} %pad_maximum_fusion), channel_id=1, source_target_pairs={{0,8},{8,16},{16,24},{24,32},{32,40},{40,48},{48,56},{56,64},{64,7... | collective-permute-start | bytes 122888 | tf_op jit(solution)/shard_map/ppermute | solution.py:270
  15.1 0.6 copy-start.2
  15.7 49.7 %copy-start.3 = (f32[32]{0:T(128)S(1)}, f32[32]{0:T(128)}, u32[]{:S(2)}) copy-start(f32[32]{0:T(128)} %param.17) | copy-start | bytes 388
  59.0 24.0 %all-to-all-start.1 = ((bf16[32,64,128]{2,1,0:T(8,128)(2,1)}), bf16[32,64,128]{2,1,0:T(8,128)(2,1)S(1)}, u32[]{:S(2)}, u32[]{:S(2)}) async-start(bf16[32,64,128]{2,1,0:T(8,128)(2,1)} %carry.1), calls=%async_computation.1 | async-start | bytes 1048576 | tf_op jit(solution)/shard_map/all_to_all | solution.py:306
  83.0 0.8 copy-start
  88.6 8.3 %collective-permute-start.1 = (bf16[264,2048]{1,0:T(8,128)(2,1)}, bf16[264,2048]{1,0:T(8,128)(2,1)S(1)}, u32[]{:S(2)}, u32[]{:S(2)}) collective-permute-start(bf16[264,2048]{1,0:T(8,128)(2,1)} %gate.1.own_ref), channel_id=1, source_target_pairs={{0,1},{1,0},{2,3},{3,2},{4,5},{5,4},{6,7},{7,6},{8,9},{9,8},{10,11... | collective-permute-start | bytes 3244040 | tf_op jit(solution)/shard_map/ppermute | solution.py:324
  96.9 23.4 %copy-start.1 = (bf16[264,2048]{1,0:T(8,128)(2,1)}, bf16[264,2048]{1,0:T(8,128)(2,1)S(1)}, u32[]{:S(2)}) copy-start(bf16[264,2048]{1,0:T(8,128)(2,1)S(1)} %collective-permute-done.1.other_ref) | copy-start | bytes 3244036
Sparse Core Ops, SparseCore 0:
  9.9 110.3 all-gather.1

commit v3 on v2

--- a/solution.py
+++ b/solution.py
@@ -4,6 +4,7 @@
 from jax.experimental import pallas as pl
 from jax.experimental.pallas import tpu as pltpu
 from jax.sharding import PartitionSpec as P
+
 
 H = 128
 P_SIZE = 64
@@ -14,6 +15,7 @@
 HALO = 8
 TAIL = 8
 EPSILON = 1e-05
+
 
 bf16 = jnp.bfloat16
 f32 = jnp.float32
@@ -201,61 +203,107 @@
         precision=lax.Precision.HIGHEST,
     )
     end = slice(BLOCK, BLOCK + TAIL)
-    out_ref[end, 2 * BLOCK :] = jnp.zeros((TAIL, within_ref.shape[1] - 2 * BLOCK), bf16)
-    for i, piece in enumerate(pieces_of(line)[0:2]):
+    for i, piece in enumerate(pieces_of(line)):
         out_ref[end, i * BLOCK : (i + 1) * BLOCK] = piece
-
-
-def turn_kernel(core_ref, w_ref, out_ref, turned_ref):
-    turned_ref[...] = w_ref[...].astype(f32).T
-    rows = out_ref.shape[0]
-    first = pl.multiple_of(core_ref[0] * rows, rows)
-    out_ref[...] = turned_ref[pl.ds(first, rows)].astype(bf16)
-
-
-def against(left, right):
-    return lax.dot_general(left, right, (((1,), (1,)), ((), ())), preferred_element_type=f32)
-
-
-def project_kernel(core_ref, own_ref, other_ref, w_ref, out_ref):
+    rest = within_ref.shape[1] - 3 * BLOCK
+    out_ref[end, 3 * BLOCK :] = jnp.zeros((TAIL, rest), bf16)
+
+
+def project_kernel(place_ref, *refs):
+    sides = (refs[0:5], refs[5:10])
+    w_refs = refs[10:12]
+    outs = refs[12:14]
+    totals = refs[14:16]
+    left_ref, done = refs[16:18]
+    k = pl.program_id(0)
+    depth = w_refs[0].shape[0]
+    tall = BLOCK + TAIL
+    half = BLOCK // 2
+    spans = ((0, 0, tall), (1, 0, tall), (2, 0, tall), (3, 0, half), (3, half, half + TAIL))
+    copies = [
+        pltpu.make_async_copy(
+            side[i], left_ref.at[step, n, pl.ds(first, count)], done.at[n, i]
+        )
+        for n, side in enumerate(sides)
+        for i, (step, first, count) in enumerate(spans)
+    ]
+
+    @pl.when(k == 0)
+    def _():
+        for i in (0, 5, 1, 6, 2, 7, 3, 8, 4, 9):
+            copies[i].start()
+
+    for step in range(4):
+
+        @pl.when(k == step)
+        def _(step=step):
+            for i in (step, 4) if step == 3 else (step,):
+                copies[i].wait()
+                copies[5 + i].wait()
+
+    @pl.when(k == 0)
+    def _():
+        for total in totals:
+            total[...] = jnp.zeros(total.shape, f32)
+
+    for r in range(2):
+        weight = jnp.concatenate(
+            [w_ref[:, (2 * j + r) * SLAB : (2 * j + r + 1) * SLAB] for w_ref in w_refs for j in range(2)],
+            axis=1,
+        )
+        at = slice(r * depth, (r + 1) * depth)
+        for n, total in enumerate(totals):
+            total[...] = total[...] + jnp.dot(
+                left_ref[k, n, 0:BLOCK, at], weight, preferred_element_type=f32
+            )
+
+    @pl.when(k == 3)
+    def _():
+        end = slice(BLOCK, tall)
+        for n, (total, out) in enumerate(zip(totals, outs)):
+            line = jnp.zeros((TAIL, BLOCK), f32)
+            for step in range(4):
+                for i in range(3):
+                    line = line + left_ref[step, n, end, i * BLOCK : (i + 1) * BLOCK].astype(f32)
+            scale = lax.rsqrt(line / (H * P_SIZE) + EPSILON)
+            column = jnp.concatenate([scale] * (SLAB // TAIL), axis=0).T[:, 0:1]
+            out[...] = (total[...] * column).astype(bf16)
+
+
+def finish_kernel(core_ref, mine_ref, theirs_ref, out_ref):
     core = core_ref[0]
-    end = slice(BLOCK, BLOCK + TAIL)
-    for seat, ref in ((core, own_ref), (1 - core, other_ref)):
-        out_ref[seat, 0:BLOCK] = against(ref[0:BLOCK], w_ref[...]).astype(bf16)
-        out_ref[seat, end] = ref[end, 0 : 2 * BLOCK]
-
-
-def finish_kernel(got_ref, out_ref):
-    sources = got_ref.shape[0]
-    end = slice(BLOCK, BLOCK + TAIL)
-    line = jnp.zeros((TAIL, BLOCK), f32)
-    for k in range(0, sources, 2):
-        for i in range(2):
-            line = line + got_ref[k, end, i * BLOCK : (i + 1) * BLOCK].astype(f32)
-    scale = lax.rsqrt(line / (H * P_SIZE) + EPSILON)
-    column = jnp.concatenate([scale] * (SLAB // TAIL), axis=0).T[:, 0:1]
-    scale = jnp.broadcast_to(column, (BLOCK, SLAB))
-    lane = lax.broadcasted_iota(jnp.int32, (BLOCK, SLAB), 1)
-    half = SLAB // 2
-    for m in range(got_ref.shape[2] // SLAB):
-        at = slice(m * SLAB, (m + 1) * SLAB)
-        sums = []
-        for d in range(2):
-            total = got_ref[d, 0:BLOCK, at].astype(f32)
-            for k in range(d + 2, sources, 2):
-                total = total + got_ref[k, 0:BLOCK, at].astype(f32)
-            sums.append(total * scale)
-        first = jnp.where(lane < half, sums[0], pltpu.roll(sums[1], half, 1))
-        second = jnp.where(lane < half, pltpu.roll(sums[0], half, 1), sums[1])
-        out_ref[:, 2 * m * SLAB : (2 * m + 1) * SLAB] = first.astype(bf16)
-        out_ref[:, (2 * m + 1) * SLAB : (2 * m + 2) * SLAB] = second.astype(bf16)
+    for j in range(mine_ref.shape[1] // SLAB):
+        at = slice(j * SLAB, (j + 1) * SLAB)
+        mine = pl.multiple_of((2 * j + core) * SLAB, SLAB)
+        theirs = pl.multiple_of((2 * j + 1 - core) * SLAB, SLAB)
+        out_ref[:, pl.ds(mine, SLAB)] = mine_ref[:, at]
+        out_ref[:, pl.ds(theirs, SLAB)] = theirs_ref[:, at]
+
+
+def seat_of(h, half, x):
+    away = (x - h) % 4
+    return (2 * h + (1 + away if half else -away)) % 8
+
+
+def weight_route(fans):
+    ring = 4
+    route = []
+    for h in range(fans):
+        for half in range(2):
+            for x in range(fans):
+                for y in range(ring):
+                    for core in range(2):
+                        source = (((2 * h + half) * ring + y) * fans + x) * 2 + core
+                        seat = seat_of(h, half, x) * ring + 2 * (y // 2) + core
+                        route.append((source, (seat * fans + h) * 2 + y % 2))
+    return route
 
 
 def whole(count):
     return [pl.BlockSpec(memory_space=pltpu.VMEM) for _ in range(count)]
 
 
-def shards(
+def layer(
     x_in, bc_in, z_in, dt_raw, dt_bias, a_log, d_skip, conv_x, conv_bc, norm_gain, out_weight
 ):
     height, width = x_in.shape
@@ -265,21 +313,14 @@
     count = lax.axis_size("seq")
     fans = lax.axis_size("head")
     core = lax.axis_index("dp")
+    mine = lax.axis_index("head")
 
     tail = jnp.concatenate([x_in[height - HALO :], bc_in[height - HALO :]], axis=1)
     halo = lax.ppermute(tail, "seq", [(i, i + 1) for i in range(count - 1)])
 
-    seat = core.astype(jnp.int32)[None]
-    piece_rows = out_weight.shape[1] // 2
-    piece = pl.pallas_call(
-        turn_kernel,
-        out_shape=jax.ShapeDtypeStruct((piece_rows, width), bf16),
-        in_specs=[pl.BlockSpec(memory_space=pltpu.SMEM)] + whole(1),
-        out_specs=whole(1)[0],
-        scratch_shapes=[pltpu.VMEM((2 * piece_rows, width), f32)],
-        name="turn",
-    )(seat, out_weight)
-    weights = lax.all_gather(piece, "seq", axis=0, tiled=True)
+    depth = width // 2
+    piece = lax.dynamic_slice_in_dim(out_weight, core * depth, depth, 0)
+    piece = lax.ppermute(piece, ("seq", "head", "dp"), weight_route(fans))
 
     xc, bcv, cols, lines, send = pl.pallas_call(
         front_kernel,
@@ -295,6 +336,7 @@
         name="front",
     )(x_in, bc_in, halo, dt_raw.T, dt_bias[None], a_log[None], conv_x, conv_bc)
 
+    weights = lax.all_gather(piece, "seq", axis=1, tiled=True)
     got = lax.all_to_all(send, "seq", 0, 0, tiled=True)
     starts = pl.pallas_call(
         scan_kernel,
@@ -321,32 +363,46 @@
         name="gate",
     )(within, state, bcv, cols, z_in, norm_gain[None])
 
-    other = lax.ppermute(ready, "dp", [(0, 1), (1, 0)])
-    share = piece_rows * count // fans
-    partial = pl.pallas_call(
+    def around(value, distance):
+        return lax.ppermute(value, "head", [((i + distance) % fans, i) for i in range(fans)])
+
+    def swapped(value):
+        return lax.ppermute(value, "dp", [(0, 1), (1, 0)])
+
+    ahead = around(ready, 1)
+    behind = around(ready, -1)
+    far_top = around(ahead[: height // 2], 1)
+    far_end = around(behind[height // 2 :], -1)
+    near = [ready, ahead, behind, far_top, far_end]
+    other = [swapped(value) for value in near]
+    away = jnp.array([0, 1, 3, 2], jnp.int32)
+    place = jnp.concatenate([(2 * mine - away) % 8, (2 * mine + 1 + away) % 8])
+    share = out_weight.shape[1] * count // fans
+    here, there = pl.pallas_call(
         project_kernel,
         grid_spec=pltpu.PrefetchScalarGridSpec(
             num_scalar_prefetch=1,
             grid=(fans,),
-            in_specs=[
-                pl.BlockSpec((height + TAIL, width), lambda j, s: (0, 0)),
-                pl.BlockSpec((height + TAIL, width), lambda j, s: (0, 0)),
-                pl.BlockSpec((share, width), lambda j, s: (j, 0)),
+            in_specs=[pl.BlockSpec(memory_space=pl.ANY)] * 10
+            + [
+                pl.BlockSpec((depth, share // 2), lambda k, s: (0, s[k])),
+                pl.BlockSpec((depth, share // 2), lambda k, s: (0, s[4 + k])),
             ],
-            out_specs=pl.BlockSpec((2, height + TAIL, share), lambda j, s: (j, 0, 0)),
+            out_specs=[pl.BlockSpec((height, share // 2), lambda k, s: (0, 0))] * 2,
+            scratch_shapes=[pltpu.VMEM((height, share // 2), f32)] * 2
+            + [pltpu.VMEM((4, 2, height + 2 * TAIL, width), bf16), pltpu.SemaphoreType.DMA((2, 5))],
         ),
-        out_shape=jax.ShapeDtypeStruct((2 * fans, height + TAIL, share), bf16),
+        out_shape=[jax.ShapeDtypeStruct((height, share // 2), bf16)] * 2,
         name="project",
-    )(seat, ready, other, weights)
-
-    swapped = lax.all_to_all(partial, ("head", "dp"), 0, 0, tiled=True)
+    )(place.astype(jnp.int32), *near, *other, weights, weights)
+
     return pl.pallas_call(
         finish_kernel,
-        out_shape=jax.ShapeDtypeStruct((height, 2 * share), bf16),
-        in_specs=whole(1),
+        out_shape=jax.ShapeDtypeStruct((height, share), bf16),
+        in_specs=[pl.BlockSpec(memory_space=pltpu.SMEM)] + whole(2),
         out_specs=whole(1)[0],
         name="finish",
-    )(swapped)
+    )(core.astype(jnp.int32)[None], here, swapped(there))
 
 
 def solution(mesh):
@@ -364,5 +420,5 @@
         P("head", "seq"),
     )
     return jax.shard_map(
-        shards, mesh=mesh, in_specs=placed, out_specs=P(("dp", "seq"), "head"), check_vma=False
+        layer, mesh=mesh, in_specs=placed, out_specs=P(("dp", "seq"), "head"), check_vma=False
     )

time: 172 us -> 174 us (1.012)
  blocking collectives: 67.1 us -> 45.1 us
  starting transfers between devices: 16.2 us -> 34.8 us
  local copies, waits for them, and re-layouts: 3.62 us -> 7.24 us
  waiting for transfers between devices: 39.1 us -> 41.5 us
    ppermute x2 -> x12, waiting for transfers between devices: 3.63 us -> 33 us  [the longest x4 25.2 us: around(): lax.ppermute(value, 'head', [((i + distance) % fans, i) for i in range(fa...]
    all_gather x1, waiting for transfers between devices: 23.4 us -> 0.02 us  [layer(): weights = lax.all_gather(piece, 'seq', axis=1, tiled=True)]
    all_to_all x2 -> x1, blocking collectives: 67.1 us -> 45.1 us  [layer(): got = lax.all_to_all(send, 'seq', 0, 0, tiled=True)]
    ppermute x2 -> x12, starting transfers between devices: 9.73 us -> 30.1 us  [the longest x6 17 us: swapped(): return lax.ppermute(value, 'dp', [(0, 1), (1, 0)])]
    all_to_all x1, waiting for transfers between devices: 12 us -> 8.47 us  [layer(): lax.all_to_all(starts, 'seq', 0, 0, tiled=True).reshape(slabs, N, SLAB)]
    unnamed x8 -> x22, local copies, waits for them, and re-layouts: 1.42 us -> 3.89 us
    all_to_all x1, starting transfers between devices: 6.44 us -> 4.63 us  [layer(): lax.all_to_all(starts, 'seq', 0, 0, tiled=True).reshape(slabs, N, SLAB)]
    pallas_call x7 -> x6, Pallas kernels: 32.1 us -> 31 us  [the longest x1 10.6 us: layer(): pl.pallas_call(project_kernel, grid_spec=pltpu.PrefetchScalarGridSpec(num...]
  transfers between devices with their start and end apart: 4 -> 14, of which waited for: 4 -> 7; matrix products, arithmetic and copies ran while one was open for 1% -> 2% of each run, Pallas kernels for 11% -> 11%
where the time goes in v3:
time: 174 us
  blocking collectives  45.1 us (26%)
  waiting for transfers between devices  41.5 us (24%)
  starting transfers between devices  34.8 us (20%)
  Pallas kernels  31 us (18%)
  between operations  13.5 us (8%)
  local copies, waits for them, and re-layouts  7.24 us (4%)
    all_to_all x1, blocking collectives, layer(): got = lax.all_to_all(send, 'seq', 0, 0, tiled=True)  45.1 us
    ppermute x4, waiting for transfers between devices, around(): lax.ppermute(value, 'head', [((i + distance) % fans, i) for i in range(fa...  25.2 us
    ppermute x6, starting transfers between devices, swapped(): return lax.ppermute(value, 'dp', [(0, 1), (1, 0)])  17 us
    pallas_call x1, Pallas kernels, layer(): pl.pallas_call(project_kernel, grid_spec=pltpu.PrefetchScalarGridSpec(num...  10.6 us
    all_to_all x1, waiting for transfers between devices, layer(): lax.all_to_all(starts, 'seq', 0, 0, tiled=True).reshape(slabs, N, SLAB)  8.47 us
    ppermute x4, starting transfers between devices, around(): lax.ppermute(value, 'head', [((i + distance) % fans, i) for i in range(fa...  7.31 us
    pallas_call x1, Pallas kernels, layer(): pl.pallas_call(front_kernel, out_shape=(jax.ShapeDtypeStruct((height, wid...  6.66 us
    pallas_call x1, Pallas kernels, layer(): pl.pallas_call(gate_kernel, out_shape=jax.ShapeDtypeStruct((height + TAIL...  4.83 us
  transfers between devices with their start and end apart: 14, of which 7 were waited for; matrix products, arithmetic and copies ran while one was open for 2% of the time, Pallas kernels for 11%

profile of v3, /device:TPU:1, one launch (start us, length us, event | category | flops | bytes accessed | tf_op | source)
XLA Modules:
  0.0 173.7 jit_solution(13650606203076306881)
XLA Ops:
  6.5 1.0 copy-done
  7.6 4.6 %collective-permute-start.10 = (bf16[1024,128]{1,0:T(8,128)(2,1)S(1)}, bf16[1024,128]{1,0:T(8,128)(2,1)S(1)}, u32[]{:S(2)}, u32[]{:S(2)}) collective-permute-start(bf16[1024,128]{1,0:T(8,128)(2,1)S(1)} %constant_dynamic-slice_fusion), channel_id=1, source_target_pairs={{0,0},{1,8},{8,1},{9,9},{16,16},{17,24},{24,17},{25,25},{2,224},{3... | collective-permute-start | bytes 786440 | tf_op jit(solution)/shard_map/ppermute | solution.py:323
  12.2 4.0 %collective-permute-done.10 = bf16[1024,128]{1,0:T(8,128)(2,1)S(1)} collective-permute-done((bf16[1024,128]{1,0:T(8,128)(2,1)S(1)}, bf16[1024,128]{1,0:T(8,128)(2,1)S(1)}, u32[]{:S(2)}, u32[]{:S(2)}) %collective-permute-start.10) | collective-permute-done | bytes 262176 | tf_op jit(solution)/shard_map/ppermute | solution.py:323
  18.4 1.3 collective-permute-start
  19.7 1.1 collective-permute-done.halo_ref
  21.4 6.7 %front.1 = (bf16[256,2048]{1,0:T(8,128)(2,1)}, bf16[256,512]{1,0:T(8,128)(2,1)}, f32[256,128]{1,0:T(8,128)}, f32[64,256]{1,0:T(8,128)}, bf16[32,72,128]{2,1,0:T(8,128)(2,1)}) custom-call(bf16[256,2048]{1,0:T(8,128)(2,1)} %x_ref.1, bf16[256,512]{1,0:T(8,128)(2,1)} %bc_ref.1, bf16[8,2560]{1,0:T(8,128)(2,1)} %copy-done.7, f32[32,256]{1,0:T(8,128)} %bitcast.7, ...), custom_call_target="tpu_custom_call" | custom-call | tf_op jit(solution)/shard_map/front/pallas_call | solution.py:325
  28.1 45.1 %all_to_all.10.got_ref = bf16[32,72,128]{2,1,0:T(8,128)(2,1)} all-to-all(bf16[32,72,128]{2,1,0:T(8,128)(2,1)} %get-tuple-element.16), channel_id=1, replica_groups=mesh['seq'=32,'head'=4,'dp'=2] {'seq'}, dimensions={0} | all-to-all | bytes 1179648 | tf_op jit(solution)/shard_map/all_to_all | solution.py:340
  73.2 2.2 %carry.1 = bf16[32,64,128]{2,1,0:T(8,128)(2,1)} custom-call(bf16[32,72,128]{2,1,0:T(8,128)(2,1)} %all_to_all.10.got_ref), custom_call_target="tpu_custom_call" | custom-call | tf_op jit(solution)/shard_map/carry/pallas_call | solution.py:341
  75.4 4.6 %all-to-all-start.1 = ((bf16[32,64,128]{2,1,0:T(8,128)(2,1)}), bf16[32,64,128]{2,1,0:T(8,128)(2,1)S(1)}, u32[]{:S(2)}, u32[]{:S(2)}) async-start(bf16[32,64,128]{2,1,0:T(8,128)(2,1)} %carry.1), calls=%async_computation.1 | async-start | bytes 1048576 | tf_op jit(solution)/shard_map/all_to_all | solution.py:348
  80.8 4.7 %within.1.within_ref = f32[256,2048]{1,0:T(8,128)} custom-call(bf16[256,2048]{1,0:T(8,128)(2,1)} %get-tuple-element.12.xc_ref, bf16[256,512]{1,0:T(8,128)(2,1)} %get-tuple-element.13.bcv_ref, f32[256,128]{1,0:T(8,128)} %get-tuple-element.14.col_ref, f32[64,256]{1,0:T(8,128)} %get-tuple-element.15.row_ref, f32[1,2048]{1,0:T(1,128)} %broadcast_in_dim_reshape.3.skip_ref), custom_call_target="tpu_custom_call" | custom-call | tf_op jit(solution)/shard_map/within/pallas_call | solution.py:350
  85.5 8.5 %all-to-all-done.1 = bf16[32,64,128]{2,1,0:T(8,128)(2,1)S(1)} async-done(((bf16[32,64,128]{2,1,0:T(8,128)(2,1)}), bf16[32,64,128]{2,1,0:T(8,128)(2,1)S(1)}, u32[]{:S(2)}, u32[]{:S(2)}) %all-to-all-start.1) | async-done | bytes 524320 | tf_op jit(solution)/shard_map/all_to_all | solution.py:348
  94.8 4.8 %gate.1.refs_0_ = bf16[264,2048]{1,0:T(8,128)(2,1)} custom-call(f32[256,2048]{1,0:T(8,128)} %within.1.within_ref, bf16[16,128,128]{2,1,0:T(8,128)(2,1)} %bitcast.6, bf16[256,512]{1,0:T(8,128)(2,1)} %get-tuple-element.13.bcv_ref, f32[256,128]{1,0:T(8,128)} %get-tuple-element.14.col_ref, bf16[256,2048]{1,0:T(8,128)(2,1)} %z_ref.1, f32[1,2048]{1,0:T(1,128)} %bitcast.8), custom_call_target="tpu_custom_call" | custom-call | tf_op jit(solution)/shard_map/gate/pallas_call | solution.py:358
  99.6 4.4 %collective-permute-start.2 = (bf16[264,2048]{1,0:T(8,128)(2,1)}, bf16[264,2048]{1,0:T(8,128)(2,1)S(1)}, u32[]{:S(2)}, u32[]{:S(2)}) collective-permute-start(bf16[264,2048]{1,0:T(8,128)(2,1)} %gate.1.refs_0_), channel_id=1, source_target_pairs={{6,0},{0,2},{2,4},{4,6},{7,1},{1,3},{3,5},{5,7},{14,8},{8,10},{10,... | collective-permute-start | bytes 3244040 | tf_op jit(solution)/shard_map/ppermute | solution.py:367
  104.0 18.3 %collective-permute-done.2.refs_2_ = bf16[264,2048]{1,0:T(8,128)(2,1)S(1)} collective-permute-done((bf16[264,2048]{1,0:T(8,128)(2,1)}, bf16[264,2048]{1,0:T(8,128)(2,1)S(1)}, u32[]{:S(2)}, u32[]{:S(2)}) %collective-permute-start.2) | collective-permute-done | bytes 1081376 | tf_op jit(solution)/shard_map/ppermute | solution.py:367
  122.3 2.3 %collective-permute-start.4 = (bf16[136,2048]{1,0:T(8,128)(2,1)S(1)}, bf16[136,2048]{1,0:T(8,128)(2,1)S(1)}, u32[]{:S(2)}, u32[]{:S(2)}) collective-permute-start(bf16[136,2048]{1,0:T(8,128)(2,1)S(1)} %slice.17), channel_id=1, source_target_pairs={{6,0},{0,2},{2,4},{4,6},{7,1},{1,3},{3,5},{5,7},{14,8},{8,10},{10,... | collective-permute-start | bytes 1671176 | tf_op jit(solution)/shard_map/ppermute | solution.py:367
  124.6 9.0 %collective-permute-start.5 = (bf16[264,2048]{1,0:T(8,128)(2,1)S(1)}, bf16[264,2048]{1,0:T(8,128)(2,1)}, u32[]{:S(2)}, u32[]{:S(2)}) collective-permute-start(bf16[264,2048]{1,0:T(8,128)(2,1)S(1)} %copy-done.1), channel_id=1, source_target_pairs={{0,1},{1,0},{2,3},{3,2},{4,5},{5,4},{6,7},{7,6},{8,9},{9,8},{10,11... | collective-permute-start | bytes 3244040 | tf_op jit(solution)/shard_map/ppermute | solution.py:370
  134.2 1.1 slice.16
  135.9 6.1 %collective-permute-start.9 = (bf16[136,2048]{1,0:T(8,128)(2,1)S(1)}, bf16[136,2048]{1,0:T(8,128)(2,1)}, u32[]{:S(2)}, u32[]{:S(2)}) collective-permute-start(bf16[136,2048]{1,0:T(8,128)(2,1)S(1)} %collective-permute-done.4.refs_4_), channel_id=1, source_target_pairs={{0,1},{1,0},{2,3},{3,2},{4,5},{5,4},{6,7},{7,6},{8,9},{9,8},{10,11... | collective-permute-start | bytes 1671176 | tf_op jit(solution)/shard_map/ppermute | solution.py:370
  142.0 6.9 %collective-permute-done.3.refs_3_ = bf16[128,2048]{1,0:T(8,128)(2,1)} collective-permute-done((bf16[128,2048]{1,0:T(8,128)(2,1)S(1)}, bf16[128,2048]{1,0:T(8,128)(2,1)}, u32[]{:S(2)}, u32[]{:S(2)}) %collective-permute-start.3) | collective-permute-done | bytes 524320 | tf_op jit(solution)/shard_map/ppermute | solution.py:367
  148.9 0.9 collective-permute-start.8
  150.4 1.3 collective-permute-done.8.refs_8_
  151.7 10.6 %project.1 = (bf16[256,512]{1,0:T(8,128)(2,1)}, bf16[256,512]{1,0:T(8,128)(2,1)}) custom-call(s32[8]{0:T(128)} %pad_add_fusion.place_ref, bf16[264,2048]{1,0:T(8,128)(2,1)} %gate.1.refs_0_, bf16[264,2048]{1,0:T(8,128)(2,1)} %collective-permute-done.1.refs_1_, bf16[264,2048]{1,0:T(8,128)(2,1)} %copy-done.2, bf16[128,2048]{1,0:T(8,128)(2,1)} %collective-permute-done.3.refs_3_, ...), custom_call_target="tpu_custom_call" | custom-call | tf_op jit(solution)/shard_map/project/pallas_call | solution.py:381
  162.8 1.4 collective-permute-done.11.theirs_ref
  164.9 2.0 %finish.1 = bf16[256,1024]{1,0:T(8,128)(2,1)} custom-call(s32[1]{0:T(128)} %bitcast.core_ref, bf16[256,512]{1,0:T(8,128)(2,1)} %get-tuple-element.17.mine_ref, bf16[256,512]{1,0:T(8,128)(2,1)} %copy-done.6), custom_call_target="tpu_custom_call" | custom-call | tf_op jit(solution)/shard_map/finish/pallas_call | solution.py:399
  (44 shorter events, 7.4 us)
Async XLA Ops:
  6.5 1.0 copy-start
  6.5 145.2 %all-gather.2.cloned.1.call-start = ((), (), s32[]{:S(2)}) async-start(), calls=%async_computation.2 | async-start | bytes 8650752 | tf_op jit(solution)/shard_map/all_gather | solution.py:339
  7.6 8.6 %collective-permute-start.10 = (bf16[1024,128]{1,0:T(8,128)(2,1)S(1)}, bf16[1024,128]{1,0:T(8,128)(2,1)S(1)}, u32[]{:S(2)}, u32[]{:S(2)}) collective-permute-start(bf16[1024,128]{1,0:T(8,128)(2,1)S(1)} %constant_dynamic-slice_fusion), channel_id=1, source_target_pairs={{0,0},{1,8},{8,1},{9,9},{16,16},{17,24},{24,17},{25,25},{2,224},{3... | collective-permute-start | bytes 786440 | tf_op jit(solution)/shard_map/ppermute | solution.py:323
  16.2 0.7 copy-start.5
  18.4 2.4 %collective-permute-start = (bf16[8,2560]{1,0:T(8,128)(2,1)S(1)}, bf16[8,2560]{1,0:T(8,128)(2,1)S(1)}, u32[]{:S(2)}, u32[]{:S(2)}) collective-permute-start(bf16[8,2560]{1,0:T(8,128)(2,1)S(1)} %pad_maximum_fusion), channel_id=1, source_target_pairs={{0,8},{8,16},{16,24},{24,32},{32,40},{40,48},{48,56},{56,64},{64,7... | collective-permute-start | bytes 122888 | tf_op jit(solution)/shard_map/ppermute | solution.py:319
  73.2 6.8 %copy-start.8 = (f32[32]{0:T(128)S(1)}, f32[32]{0:T(128)}, u32[]{:S(2)}) copy-start(f32[32]{0:T(128)} %param.18) | copy-start | bytes 388
  75.4 18.6 %all-to-all-start.1 = ((bf16[32,64,128]{2,1,0:T(8,128)(2,1)}), bf16[32,64,128]{2,1,0:T(8,128)(2,1)S(1)}, u32[]{:S(2)}, u32[]{:S(2)}) async-start(bf16[32,64,128]{2,1,0:T(8,128)(2,1)} %carry.1), calls=%async_computation.1 | async-start | bytes 1048576 | tf_op jit(solution)/shard_map/all_to_all | solution.py:348
  94.0 0.8 copy-start.3
  99.6 25.0 %copy-start.1 = (bf16[264,2048]{1,0:T(8,128)(2,1)S(1)}, bf16[264,2048]{1,0:T(8,128)(2,1)}, u32[]{:S(2)}) copy-start(bf16[264,2048]{1,0:T(8,128)(2,1)} %gate.1.refs_0_) | copy-start | bytes 3244036
  99.6 50.2 %copy-start.9 = (s32[4]{0:T(128)S(1)}, s32[4]{0:T(128)}, u32[]{:S(2)}) copy-start(s32[4]{0:T(128)} %constant.40) | copy-start | bytes 52
  99.6 50.2 %copy-start.10 = (s32[4]{0:T(128)S(1)}, s32[4]{0:T(128)}, u32[]{:S(2)}) copy-start(s32[4]{0:T(128)} %constant.39.clone) | copy-start | bytes 52
  99.6 22.7 %collective-permute-start.2 = (bf16[264,2048]{1,0:T(8,128)(2,1)}, bf16[264,2048]{1,0:T(8,128)(2,1)S(1)}, u32[]{:S(2)}, u32[]{:S(2)}) collective-permute-start(bf16[264,2048]{1,0:T(8,128)(2,1)} %gate.1.refs_0_), channel_id=1, source_target_pairs={{6,0},{0,2},{2,4},{4,6},{7,1},{1,3},{3,5},{5,7},{14,8},{8,10},{10,... | collective-permute-start | bytes 3244040 | tf_op jit(solution)/shard_map/ppermute | solution.py:367
  104.0 29.7 %collective-permute-start.1 = (bf16[264,2048]{1,0:T(8,128)(2,1)}, bf16[264,2048]{1,0:T(8,128)(2,1)}, u32[]{:S(2)}, u32[]{:S(2)}) collective-permute-start(bf16[264,2048]{1,0:T(8,128)(2,1)} %gate.1.refs_0_), channel_id=1, source_target_pairs={{2,0},{4,2},{6,4},{0,6},{3,1},{5,3},{7,5},{1,7},{10,8},{12,10},{14... | collective-permute-start | bytes 3244040 | tf_op jit(solution)/shard_map/ppermute | solution.py:367
  122.3 13.0 %copy-start.2 = (bf16[264,2048]{1,0:T(8,128)(2,1)}, bf16[264,2048]{1,0:T(8,128)(2,1)S(1)}, u32[]{:S(2)}) copy-start(bf16[264,2048]{1,0:T(8,128)(2,1)S(1)} %collective-permute-done.2.refs_2_) | copy-start | bytes 3244036
  122.3 13.6 %collective-permute-start.4 = (bf16[136,2048]{1,0:T(8,128)(2,1)S(1)}, bf16[136,2048]{1,0:T(8,128)(2,1)S(1)}, u32[]{:S(2)}, u32[]{:S(2)}) collective-permute-start(bf16[136,2048]{1,0:T(8,128)(2,1)S(1)} %slice.17), channel_id=1, source_target_pairs={{6,0},{0,2},{2,4},{4,6},{7,1},{1,3},{3,5},{5,7},{14,8},{8,10},{10,... | collective-permute-start | bytes 1671176 | tf_op jit(solution)/shard_map/ppermute | solution.py:367
  124.6 25.8 %collective-permute-start.5 = (bf16[264,2048]{1,0:T(8,128)(2,1)S(1)}, bf16[264,2048]{1,0:T(8,128)(2,1)}, u32[]{:S(2)}, u32[]{:S(2)}) collective-permute-start(bf16[264,2048]{1,0:T(8,128)(2,1)S(1)} %copy-done.1), channel_id=1, source_target_pairs={{0,1},{1,0},{2,3},{3,2},{4,5},{5,4},{6,7},{7,6},{8,9},{9,8},{10,11... | collective-permute-start | bytes 3244040 | tf_op jit(solution)/shard_map/ppermute | solution.py:370
  133.7 18.0 %collective-permute-start.7 = (bf16[264,2048]{1,0:T(8,128)(2,1)S(1)}, bf16[264,2048]{1,0:T(8,128)(2,1)}, u32[]{:S(2)}, u32[]{:S(2)}) collective-permute-start(bf16[264,2048]{1,0:T(8,128)(2,1)S(1)} %collective-permute-done.2.refs_2_), channel_id=1, source_target_pairs={{0,1},{1,0},{2,3},{3,2},{4,5},{5,4},{6,7},{7,6},{8,9},{9,8},{10,11... | collective-permute-start | bytes 3244040 | tf_op jit(solution)/shard_map/ppermute | solution.py:370
  133.7 18.0 %collective-permute-start.6 = (bf16[264,2048]{1,0:T(8,128)(2,1)}, bf16[264,2048]{1,0:T(8,128)(2,1)}, u32[]{:S(2)}, u32[]{:S(2)}) collective-permute-start(bf16[264,2048]{1,0:T(8,128)(2,1)} %collective-permute-done.1.refs_1_), channel_id=1, source_target_pairs={{0,1},{1,0},{2,3},{3,2},{4,5},{5,4},{6,7},{7,6},{8,9},{9,8},{10,11... | collective-permute-start | bytes 3244040 | tf_op jit(solution)/shard_map/ppermute | solution.py:370
  135.3 13.7 %collective-permute-start.3 = (bf16[128,2048]{1,0:T(8,128)(2,1)S(1)}, bf16[128,2048]{1,0:T(8,128)(2,1)}, u32[]{:S(2)}, u32[]{:S(2)}) collective-permute-start(bf16[128,2048]{1,0:T(8,128)(2,1)S(1)} %slice.16), channel_id=1, source_target_pairs={{2,0},{4,2},{6,4},{0,6},{3,1},{5,3},{7,5},{1,7},{10,8},{12,10},{14... | collective-permute-start | bytes 1572872 | tf_op jit(solution)/shard_map/ppermute | solution.py:367
  135.9 15.8 %copy-start.4 = (bf16[136,2048]{1,0:T(8,128)(2,1)}, bf16[136,2048]{1,0:T(8,128)(2,1)S(1)}, u32[]{:S(2)}) copy-start(bf16[136,2048]{1,0:T(8,128)(2,1)S(1)} %collective-permute-done.4.refs_4_) | copy-start | bytes 1671172
  135.9 15.8 %collective-permute-start.9 = (bf16[136,2048]{1,0:T(8,128)(2,1)S(1)}, bf16[136,2048]{1,0:T(8,128)(2,1)}, u32[]{:S(2)}, u32[]{:S(2)}) collective-permute-start(bf16[136,2048]{1,0:T(8,128)(2,1)S(1)} %collective-permute-done.4.refs_4_), channel_id=1, source_target_pairs={{0,1},{1,0},{2,3},{3,2},{4,5},{5,4},{6,7},{7,6},{8,9},{9,8},{10,11... | collective-permute-start | bytes 1671176 | tf_op jit(solution)/shard_map/ppermute | solution.py:370
  148.9 2.7 %collective-permute-start.8 = (bf16[128,2048]{1,0:T(8,128)(2,1)}, bf16[128,2048]{1,0:T(8,128)(2,1)}, u32[]{:S(2)}, u32[]{:S(2)}) collective-permute-start(bf16[128,2048]{1,0:T(8,128)(2,1)} %collective-permute-done.3.refs_3_), channel_id=1, source_target_pairs={{0,1},{1,0},{2,3},{3,2},{4,5},{5,4},{6,7},{7,6},{8,9},{9,8},{10,11... | collective-permute-start | bytes 1572872 | tf_op jit(solution)/shard_map/ppermute | solution.py:370
  162.4 1.8 %collective-permute-start.11 = (bf16[256,512]{1,0:T(8,128)(2,1)}, bf16[256,512]{1,0:T(8,128)(2,1)S(1)}, u32[]{:S(2)}, u32[]{:S(2)}) collective-permute-start(bf16[256,512]{1,0:T(8,128)(2,1)} %get-tuple-element.18), channel_id=1, source_target_pairs={{0,1},{1,0},{2,3},{3,2},{4,5},{5,4},{6,7},{7,6},{8,9},{9,8},{10,11... | collective-permute-start | bytes 786440 | tf_op jit(solution)/shard_map/ppermute | solution.py:370
  164.2 0.7 copy-start.6
  (1 other events, 0.6 us)
Sparse Core Ops, SparseCore 0:
  17.1 123.2 all-gather.1

commit v4 on v3

--- a/solution.py
+++ b/solution.py
@@ -213,61 +213,76 @@
     sides = (refs[0:5], refs[5:10])
     w_refs = refs[10:12]
     outs = refs[12:14]
-    totals = refs[14:16]
-    left_ref, done = refs[16:18]
+    total, left_ref, tail_ref, done = refs[14:18]
     k = pl.program_id(0)
-    depth = w_refs[0].shape[0]
-    tall = BLOCK + TAIL
     half = BLOCK // 2
-    spans = ((0, 0, tall), (1, 0, tall), (2, 0, tall), (3, 0, half), (3, half, half + TAIL))
-    copies = [
-        pltpu.make_async_copy(
-            side[i], left_ref.at[step, n, pl.ds(first, count)], done.at[n, i]
-        )
-        for n, side in enumerate(sides)
-        for i, (step, first, count) in enumerate(spans)
-    ]
+    bodies, tails = [], []
+    for n, side in enumerate(sides):
+        first = n * BLOCK
+        rows = [(i, 0, BLOCK, first) for i in range(3)]
+        rows += [(3, 0, half, first), (4, 0, half, first + half)]
+        for i, (ref, start, count, at) in enumerate(rows):
+            step = min(i, 3)
+            bodies.append(
+                (step, pltpu.make_async_copy(
+                    side[ref].at[pl.ds(start, count)],
+                    left_ref.at[step, pl.ds(at, count)],
+                    done.at[n, i],
+                ))
+            )
+        for step, (ref, start) in enumerate(((0, BLOCK), (1, BLOCK), (2, BLOCK), (4, half))):
+            tails.append(
+                pltpu.make_async_copy(
+                    side[ref].at[pl.ds(start, TAIL)], tail_ref.at[step, n], done.at[n, 5 + step]
+                )
+            )
 
     @pl.when(k == 0)
     def _():
-        for i in (0, 5, 1, 6, 2, 7, 3, 8, 4, 9):
-            copies[i].start()
+        for step in range(4):
+            for own, copy in bodies:
+                if own == step:
+                    copy.start()
+        for copy in tails:
+            copy.start()
+        total[...] = jnp.zeros(total.shape, f32)
 
     for step in range(4):
 
         @pl.when(k == step)
         def _(step=step):
-            for i in (step, 4) if step == 3 else (step,):
-                copies[i].wait()
-                copies[5 + i].wait()
-
-    @pl.when(k == 0)
-    def _():
-        for total in totals:
-            total[...] = jnp.zeros(total.shape, f32)
-
-    for r in range(2):
-        weight = jnp.concatenate(
-            [w_ref[:, (2 * j + r) * SLAB : (2 * j + r + 1) * SLAB] for w_ref in w_refs for j in range(2)],
-            axis=1,
-        )
-        at = slice(r * depth, (r + 1) * depth)
-        for n, total in enumerate(totals):
-            total[...] = total[...] + jnp.dot(
-                left_ref[k, n, 0:BLOCK, at], weight, preferred_element_type=f32
+            for own, copy in bodies:
+                if own == step:
+                    copy.wait()
+
+    weight = jnp.concatenate(
+        [
+            jnp.concatenate(
+                [
+                    w_ref[:, (2 * j + r) * SLAB : (2 * j + r + 1) * SLAB]
+                    for w_ref in w_refs
+                    for j in range(2)
+                ],
+                axis=1,
             )
+            for r in range(2)
+        ],
+        axis=0,
+    )
+    total[...] = total[...] + jnp.dot(left_ref[k], weight, preferred_element_type=f32)
 
     @pl.when(k == 3)
     def _():
-        end = slice(BLOCK, tall)
-        for n, (total, out) in enumerate(zip(totals, outs)):
+        for copy in tails:
+            copy.wait()
+        for n, out in enumerate(outs):
             line = jnp.zeros((TAIL, BLOCK), f32)
             for step in range(4):
                 for i in range(3):
-                    line = line + left_ref[step, n, end, i * BLOCK : (i + 1) * BLOCK].astype(f32)
+                    line = line + tail_ref[step, n, :, i * BLOCK : (i + 1) * BLOCK].astype(f32)
             scale = lax.rsqrt(line / (H * P_SIZE) + EPSILON)
             column = jnp.concatenate([scale] * (SLAB // TAIL), axis=0).T[:, 0:1]
-            out[...] = (total[...] * column).astype(bf16)
+            out[...] = (total[n * BLOCK : (n + 1) * BLOCK] * column).astype(bf16)
 
 
 def finish_kernel(core_ref, mine_ref, theirs_ref, out_ref):
@@ -389,8 +404,12 @@
                 pl.BlockSpec((depth, share // 2), lambda k, s: (0, s[4 + k])),
             ],
             out_specs=[pl.BlockSpec((height, share // 2), lambda k, s: (0, 0))] * 2,
-            scratch_shapes=[pltpu.VMEM((height, share // 2), f32)] * 2
-            + [pltpu.VMEM((4, 2, height + 2 * TAIL, width), bf16), pltpu.SemaphoreType.DMA((2, 5))],
+            scratch_shapes=[
+                pltpu.VMEM((2 * height, share // 2), f32),
+                pltpu.VMEM((4, 2 * height, width), bf16),
+                pltpu.VMEM((4, 2, TAIL, width), bf16),
+                pltpu.SemaphoreType.DMA((2, 9)),
+            ],
         ),
         out_shape=[jax.ShapeDtypeStruct((height, share // 2), bf16)] * 2,
         name="project",

time: 174 us -> 174 us (level)
  no operation moved by 1% of the time
where the time goes in v4:
time: 174 us
  blocking collectives  45.1 us (26%)
  waiting for transfers between devices  41.5 us (24%)
  starting transfers between devices  34.8 us (20%)
  Pallas kernels  31.1 us (18%)
  between operations  13.5 us (8%)
  local copies, waits for them, and re-layouts  7.25 us (4%)
    all_to_all x1, blocking collectives, layer(): got = lax.all_to_all(send, 'seq', 0, 0, tiled=True)  45.1 us
    ppermute x4, waiting for transfers between devices, around(): lax.ppermute(value, 'head', [((i + distance) % fans, i) for i in range(fa...  25.2 us
    ppermute x6, starting transfers between devices, swapped(): return lax.ppermute(value, 'dp', [(0, 1), (1, 0)])  17 us
    pallas_call x1, Pallas kernels, layer(): pl.pallas_call(project_kernel, grid_spec=pltpu.PrefetchScalarGridSpec(num...  10.7 us
    all_to_all x1, waiting for transfers between devices, layer(): lax.all_to_all(starts, 'seq', 0, 0, tiled=True).reshape(slabs, N, SLAB)  8.47 us
    ppermute x4, starting transfers between devices, around(): lax.ppermute(value, 'head', [((i + distance) % fans, i) for i in range(fa...  7.31 us
    pallas_call x1, Pallas kernels, layer(): pl.pallas_call(front_kernel, out_shape=(jax.ShapeDtypeStruct((height, wid...  6.66 us
    pallas_call x1, Pallas kernels, layer(): pl.pallas_call(gate_kernel, out_shape=jax.ShapeDtypeStruct((height + TAIL...  4.83 us
  transfers between devices with their start and end apart: 14, of which 7 were waited for; matrix products, arithmetic and copies ran while one was open for 2% of the time, Pallas kernels for 11%

profile of v4, /device:TPU:1, one launch (start us, length us, event | category | flops | bytes accessed | tf_op | source)
XLA Modules:
  0.0 173.7 jit_solution(6257145114778789404)
XLA Ops:
  6.5 1.0 copy-done
  7.6 4.6 %collective-permute-start.10 = (bf16[1024,128]{1,0:T(8,128)(2,1)S(1)}, bf16[1024,128]{1,0:T(8,128)(2,1)S(1)}, u32[]{:S(2)}, u32[]{:S(2)}) collective-permute-start(bf16[1024,128]{1,0:T(8,128)(2,1)S(1)} %constant_dynamic-slice_fusion), channel_id=1, source_target_pairs={{0,0},{1,8},{8,1},{9,9},{16,16},{17,24},{24,17},{25,25},{2,224},{3... | collective-permute-start | bytes 786440 | tf_op jit(solution)/shard_map/ppermute | solution.py:338
  12.2 4.0 %collective-permute-done.10 = bf16[1024,128]{1,0:T(8,128)(2,1)S(1)} collective-permute-done((bf16[1024,128]{1,0:T(8,128)(2,1)S(1)}, bf16[1024,128]{1,0:T(8,128)(2,1)S(1)}, u32[]{:S(2)}, u32[]{:S(2)}) %collective-permute-start.10) | collective-permute-done | bytes 262176 | tf_op jit(solution)/shard_map/ppermute | solution.py:338
  18.4 1.3 collective-permute-start
  19.7 1.1 collective-permute-done.halo_ref
  21.4 6.7 %front.1 = (bf16[256,2048]{1,0:T(8,128)(2,1)}, bf16[256,512]{1,0:T(8,128)(2,1)}, f32[256,128]{1,0:T(8,128)}, f32[64,256]{1,0:T(8,128)}, bf16[32,72,128]{2,1,0:T(8,128)(2,1)}) custom-call(bf16[256,2048]{1,0:T(8,128)(2,1)} %x_ref.1, bf16[256,512]{1,0:T(8,128)(2,1)} %bc_ref.1, bf16[8,2560]{1,0:T(8,128)(2,1)} %copy-done.7, f32[32,256]{1,0:T(8,128)} %bitcast.7, ...), custom_call_target="tpu_custom_call" | custom-call | tf_op jit(solution)/shard_map/front/pallas_call | solution.py:340
  28.1 45.1 %all_to_all.10.got_ref = bf16[32,72,128]{2,1,0:T(8,128)(2,1)} all-to-all(bf16[32,72,128]{2,1,0:T(8,128)(2,1)} %get-tuple-element.16), channel_id=1, replica_groups=mesh['seq'=32,'head'=4,'dp'=2] {'seq'}, dimensions={0} | all-to-all | bytes 1179648 | tf_op jit(solution)/shard_map/all_to_all | solution.py:355
  73.2 2.2 %carry.1 = bf16[32,64,128]{2,1,0:T(8,128)(2,1)} custom-call(bf16[32,72,128]{2,1,0:T(8,128)(2,1)} %all_to_all.10.got_ref), custom_call_target="tpu_custom_call" | custom-call | tf_op jit(solution)/shard_map/carry/pallas_call | solution.py:356
  75.4 4.6 %all-to-all-start.1 = ((bf16[32,64,128]{2,1,0:T(8,128)(2,1)}), bf16[32,64,128]{2,1,0:T(8,128)(2,1)S(1)}, u32[]{:S(2)}, u32[]{:S(2)}) async-start(bf16[32,64,128]{2,1,0:T(8,128)(2,1)} %carry.1), calls=%async_computation.1 | async-start | bytes 1048576 | tf_op jit(solution)/shard_map/all_to_all | solution.py:363
  80.8 4.7 %within.1.within_ref = f32[256,2048]{1,0:T(8,128)} custom-call(bf16[256,2048]{1,0:T(8,128)(2,1)} %get-tuple-element.12.xc_ref, bf16[256,512]{1,0:T(8,128)(2,1)} %get-tuple-element.13.bcv_ref, f32[256,128]{1,0:T(8,128)} %get-tuple-element.14.col_ref, f32[64,256]{1,0:T(8,128)} %get-tuple-element.15.row_ref, f32[1,2048]{1,0:T(1,128)} %broadcast_in_dim_reshape.3.skip_ref), custom_call_target="tpu_custom_call" | custom-call | tf_op jit(solution)/shard_map/within/pallas_call | solution.py:365
  85.5 8.5 %all-to-all-done.1 = bf16[32,64,128]{2,1,0:T(8,128)(2,1)S(1)} async-done(((bf16[32,64,128]{2,1,0:T(8,128)(2,1)}), bf16[32,64,128]{2,1,0:T(8,128)(2,1)S(1)}, u32[]{:S(2)}, u32[]{:S(2)}) %all-to-all-start.1) | async-done | bytes 524320 | tf_op jit(solution)/shard_map/all_to_all | solution.py:363
  94.8 4.8 %gate.1.refs_0_ = bf16[264,2048]{1,0:T(8,128)(2,1)} custom-call(f32[256,2048]{1,0:T(8,128)} %within.1.within_ref, bf16[16,128,128]{2,1,0:T(8,128)(2,1)} %bitcast.6, bf16[256,512]{1,0:T(8,128)(2,1)} %get-tuple-element.13.bcv_ref, f32[256,128]{1,0:T(8,128)} %get-tuple-element.14.col_ref, bf16[256,2048]{1,0:T(8,128)(2,1)} %z_ref.1, f32[1,2048]{1,0:T(1,128)} %bitcast.8), custom_call_target="tpu_custom_call" | custom-call | tf_op jit(solution)/shard_map/gate/pallas_call | solution.py:373
  99.6 4.4 %collective-permute-start.2 = (bf16[264,2048]{1,0:T(8,128)(2,1)}, bf16[264,2048]{1,0:T(8,128)(2,1)S(1)}, u32[]{:S(2)}, u32[]{:S(2)}) collective-permute-start(bf16[264,2048]{1,0:T(8,128)(2,1)} %gate.1.refs_0_), channel_id=1, source_target_pairs={{6,0},{0,2},{2,4},{4,6},{7,1},{1,3},{3,5},{5,7},{14,8},{8,10},{10,... | collective-permute-start | bytes 3244040 | tf_op jit(solution)/shard_map/ppermute | solution.py:382
  104.0 18.3 %collective-permute-done.2.refs_2_ = bf16[264,2048]{1,0:T(8,128)(2,1)S(1)} collective-permute-done((bf16[264,2048]{1,0:T(8,128)(2,1)}, bf16[264,2048]{1,0:T(8,128)(2,1)S(1)}, u32[]{:S(2)}, u32[]{:S(2)}) %collective-permute-start.2) | collective-permute-done | bytes 1081376 | tf_op jit(solution)/shard_map/ppermute | solution.py:382
  122.3 2.3 %collective-permute-start.4 = (bf16[136,2048]{1,0:T(8,128)(2,1)S(1)}, bf16[136,2048]{1,0:T(8,128)(2,1)S(1)}, u32[]{:S(2)}, u32[]{:S(2)}) collective-permute-start(bf16[136,2048]{1,0:T(8,128)(2,1)S(1)} %slice.17), channel_id=1, source_target_pairs={{6,0},{0,2},{2,4},{4,6},{7,1},{1,3},{3,5},{5,7},{14,8},{8,10},{10,... | collective-permute-start | bytes 1671176 | tf_op jit(solution)/shard_map/ppermute | solution.py:382
  124.6 9.0 %collective-permute-start.5 = (bf16[264,2048]{1,0:T(8,128)(2,1)S(1)}, bf16[264,2048]{1,0:T(8,128)(2,1)}, u32[]{:S(2)}, u32[]{:S(2)}) collective-permute-start(bf16[264,2048]{1,0:T(8,128)(2,1)S(1)} %copy-done.1), channel_id=1, source_target_pairs={{0,1},{1,0},{2,3},{3,2},{4,5},{5,4},{6,7},{7,6},{8,9},{9,8},{10,11... | collective-permute-start | bytes 3244040 | tf_op jit(solution)/shard_map/ppermute | solution.py:385
  134.2 1.1 slice.16
  135.9 6.1 %collective-permute-start.9 = (bf16[136,2048]{1,0:T(8,128)(2,1)S(1)}, bf16[136,2048]{1,0:T(8,128)(2,1)}, u32[]{:S(2)}, u32[]{:S(2)}) collective-permute-start(bf16[136,2048]{1,0:T(8,128)(2,1)S(1)} %collective-permute-done.4.refs_4_), channel_id=1, source_target_pairs={{0,1},{1,0},{2,3},{3,2},{4,5},{5,4},{6,7},{7,6},{8,9},{9,8},{10,11... | collective-permute-start | bytes 1671176 | tf_op jit(solution)/shard_map/ppermute | solution.py:385
  142.0 6.9 %collective-permute-done.3.refs_3_ = bf16[128,2048]{1,0:T(8,128)(2,1)} collective-permute-done((bf16[128,2048]{1,0:T(8,128)(2,1)S(1)}, bf16[128,2048]{1,0:T(8,128)(2,1)}, u32[]{:S(2)}, u32[]{:S(2)}) %collective-permute-start.3) | collective-permute-done | bytes 524320 | tf_op jit(solution)/shard_map/ppermute | solution.py:382
  148.9 0.9 collective-permute-start.8
  150.4 1.3 collective-permute-done.8.refs_8_
  151.7 10.7 %project.1 = (bf16[256,512]{1,0:T(8,128)(2,1)}, bf16[256,512]{1,0:T(8,128)(2,1)}) custom-call(s32[8]{0:T(128)} %pad_add_fusion.place_ref, bf16[264,2048]{1,0:T(8,128)(2,1)} %gate.1.refs_0_, bf16[264,2048]{1,0:T(8,128)(2,1)} %collective-permute-done.1.refs_1_, bf16[264,2048]{1,0:T(8,128)(2,1)} %copy-done.2, bf16[128,2048]{1,0:T(8,128)(2,1)} %collective-permute-done.3.refs_3_, ...), custom_call_target="tpu_custom_call" | custom-call | tf_op jit(solution)/shard_map/project/pallas_call | solution.py:396
  162.8 1.4 collective-permute-done.11.theirs_ref
  164.9 2.0 %finish.1 = bf16[256,1024]{1,0:T(8,128)(2,1)} custom-call(s32[1]{0:T(128)} %bitcast.core_ref, bf16[256,512]{1,0:T(8,128)(2,1)} %get-tuple-element.17.mine_ref, bf16[256,512]{1,0:T(8,128)(2,1)} %copy-done.6), custom_call_target="tpu_custom_call" | custom-call | tf_op jit(solution)/shard_map/finish/pallas_call | solution.py:418
  (44 shorter events, 7.4 us)
Async XLA Ops:
  6.5 1.0 copy-start
  6.5 145.2 %all-gather.2.cloned.1.call-start = ((), (), s32[]{:S(2)}) async-start(), calls=%async_computation.2 | async-start | bytes 8650752 | tf_op jit(solution)/shard_map/all_gather | solution.py:354
  7.6 8.6 %collective-permute-start.10 = (bf16[1024,128]{1,0:T(8,128)(2,1)S(1)}, bf16[1024,128]{1,0:T(8,128)(2,1)S(1)}, u32[]{:S(2)}, u32[]{:S(2)}) collective-permute-start(bf16[1024,128]{1,0:T(8,128)(2,1)S(1)} %constant_dynamic-slice_fusion), channel_id=1, source_target_pairs={{0,0},{1,8},{8,1},{9,9},{16,16},{17,24},{24,17},{25,25},{2,224},{3... | collective-permute-start | bytes 786440 | tf_op jit(solution)/shard_map/ppermute | solution.py:338
  16.2 0.7 copy-start.5
  18.4 2.4 %collective-permute-start = (bf16[8,2560]{1,0:T(8,128)(2,1)S(1)}, bf16[8,2560]{1,0:T(8,128)(2,1)S(1)}, u32[]{:S(2)}, u32[]{:S(2)}) collective-permute-start(bf16[8,2560]{1,0:T(8,128)(2,1)S(1)} %pad_maximum_fusion), channel_id=1, source_target_pairs={{0,8},{8,16},{16,24},{24,32},{32,40},{40,48},{48,56},{56,64},{64,7... | collective-permute-start | bytes 122888 | tf_op jit(solution)/shard_map/ppermute | solution.py:334
  73.2 6.8 %copy-start.8 = (f32[32]{0:T(128)S(1)}, f32[32]{0:T(128)}, u32[]{:S(2)}) copy-start(f32[32]{0:T(128)} %param.18) | copy-start | bytes 388
  75.4 18.6 %all-to-all-start.1 = ((bf16[32,64,128]{2,1,0:T(8,128)(2,1)}), bf16[32,64,128]{2,1,0:T(8,128)(2,1)S(1)}, u32[]{:S(2)}, u32[]{:S(2)}) async-start(bf16[32,64,128]{2,1,0:T(8,128)(2,1)} %carry.1), calls=%async_computation.1 | async-start | bytes 1048576 | tf_op jit(solution)/shard_map/all_to_all | solution.py:363
  94.0 0.8 copy-start.3
  99.6 25.0 %copy-start.1 = (bf16[264,2048]{1,0:T(8,128)(2,1)S(1)}, bf16[264,2048]{1,0:T(8,128)(2,1)}, u32[]{:S(2)}) copy-start(bf16[264,2048]{1,0:T(8,128)(2,1)} %gate.1.refs_0_) | copy-start | bytes 3244036
  99.6 50.2 %copy-start.9 = (s32[4]{0:T(128)S(1)}, s32[4]{0:T(128)}, u32[]{:S(2)}) copy-start(s32[4]{0:T(128)} %constant.40) | copy-start | bytes 52
  99.6 50.2 %copy-start.10 = (s32[4]{0:T(128)S(1)}, s32[4]{0:T(128)}, u32[]{:S(2)}) copy-start(s32[4]{0:T(128)} %constant.39.clone) | copy-start | bytes 52
  99.6 22.7 %collective-permute-start.2 = (bf16[264,2048]{1,0:T(8,128)(2,1)}, bf16[264,2048]{1,0:T(8,128)(2,1)S(1)}, u32[]{:S(2)}, u32[]{:S(2)}) collective-permute-start(bf16[264,2048]{1,0:T(8,128)(2,1)} %gate.1.refs_0_), channel_id=1, source_target_pairs={{6,0},{0,2},{2,4},{4,6},{7,1},{1,3},{3,5},{5,7},{14,8},{8,10},{10,... | collective-permute-start | bytes 3244040 | tf_op jit(solution)/shard_map/ppermute | solution.py:382
  104.0 29.7 %collective-permute-start.1 = (bf16[264,2048]{1,0:T(8,128)(2,1)}, bf16[264,2048]{1,0:T(8,128)(2,1)}, u32[]{:S(2)}, u32[]{:S(2)}) collective-permute-start(bf16[264,2048]{1,0:T(8,128)(2,1)} %gate.1.refs_0_), channel_id=1, source_target_pairs={{2,0},{4,2},{6,4},{0,6},{3,1},{5,3},{7,5},{1,7},{10,8},{12,10},{14... | collective-permute-start | bytes 3244040 | tf_op jit(solution)/shard_map/ppermute | solution.py:382
  122.3 13.0 %copy-start.2 = (bf16[264,2048]{1,0:T(8,128)(2,1)}, bf16[264,2048]{1,0:T(8,128)(2,1)S(1)}, u32[]{:S(2)}) copy-start(bf16[264,2048]{1,0:T(8,128)(2,1)S(1)} %collective-permute-done.2.refs_2_) | copy-start | bytes 3244036
  122.3 13.6 %collective-permute-start.4 = (bf16[136,2048]{1,0:T(8,128)(2,1)S(1)}, bf16[136,2048]{1,0:T(8,128)(2,1)S(1)}, u32[]{:S(2)}, u32[]{:S(2)}) collective-permute-start(bf16[136,2048]{1,0:T(8,128)(2,1)S(1)} %slice.17), channel_id=1, source_target_pairs={{6,0},{0,2},{2,4},{4,6},{7,1},{1,3},{3,5},{5,7},{14,8},{8,10},{10,... | collective-permute-start | bytes 1671176 | tf_op jit(solution)/shard_map/ppermute | solution.py:382
  124.6 25.8 %collective-permute-start.5 = (bf16[264,2048]{1,0:T(8,128)(2,1)S(1)}, bf16[264,2048]{1,0:T(8,128)(2,1)}, u32[]{:S(2)}, u32[]{:S(2)}) collective-permute-start(bf16[264,2048]{1,0:T(8,128)(2,1)S(1)} %copy-done.1), channel_id=1, source_target_pairs={{0,1},{1,0},{2,3},{3,2},{4,5},{5,4},{6,7},{7,6},{8,9},{9,8},{10,11... | collective-permute-start | bytes 3244040 | tf_op jit(solution)/shard_map/ppermute | solution.py:385
  133.7 18.0 %collective-permute-start.7 = (bf16[264,2048]{1,0:T(8,128)(2,1)S(1)}, bf16[264,2048]{1,0:T(8,128)(2,1)}, u32[]{:S(2)}, u32[]{:S(2)}) collective-permute-start(bf16[264,2048]{1,0:T(8,128)(2,1)S(1)} %collective-permute-done.2.refs_2_), channel_id=1, source_target_pairs={{0,1},{1,0},{2,3},{3,2},{4,5},{5,4},{6,7},{7,6},{8,9},{9,8},{10,11... | collective-permute-start | bytes 3244040 | tf_op jit(solution)/shard_map/ppermute | solution.py:385
  133.7 18.0 %collective-permute-start.6 = (bf16[264,2048]{1,0:T(8,128)(2,1)}, bf16[264,2048]{1,0:T(8,128)(2,1)}, u32[]{:S(2)}, u32[]{:S(2)}) collective-permute-start(bf16[264,2048]{1,0:T(8,128)(2,1)} %collective-permute-done.1.refs_1_), channel_id=1, source_target_pairs={{0,1},{1,0},{2,3},{3,2},{4,5},{5,4},{6,7},{7,6},{8,9},{9,8},{10,11... | collective-permute-start | bytes 3244040 | tf_op jit(solution)/shard_map/ppermute | solution.py:385
  135.3 13.7 %collective-permute-start.3 = (bf16[128,2048]{1,0:T(8,128)(2,1)S(1)}, bf16[128,2048]{1,0:T(8,128)(2,1)}, u32[]{:S(2)}, u32[]{:S(2)}) collective-permute-start(bf16[128,2048]{1,0:T(8,128)(2,1)S(1)} %slice.16), channel_id=1, source_target_pairs={{2,0},{4,2},{6,4},{0,6},{3,1},{5,3},{7,5},{1,7},{10,8},{12,10},{14... | collective-permute-start | bytes 1572872 | tf_op jit(solution)/shard_map/ppermute | solution.py:382
  135.9 15.8 %copy-start.4 = (bf16[136,2048]{1,0:T(8,128)(2,1)}, bf16[136,2048]{1,0:T(8,128)(2,1)S(1)}, u32[]{:S(2)}) copy-start(bf16[136,2048]{1,0:T(8,128)(2,1)S(1)} %collective-permute-done.4.refs_4_) | copy-start | bytes 1671172
  135.9 15.8 %collective-permute-start.9 = (bf16[136,2048]{1,0:T(8,128)(2,1)S(1)}, bf16[136,2048]{1,0:T(8,128)(2,1)}, u32[]{:S(2)}, u32[]{:S(2)}) collective-permute-start(bf16[136,2048]{1,0:T(8,128)(2,1)S(1)} %collective-permute-done.4.refs_4_), channel_id=1, source_target_pairs={{0,1},{1,0},{2,3},{3,2},{4,5},{5,4},{6,7},{7,6},{8,9},{9,8},{10,11... | collective-permute-start | bytes 1671176 | tf_op jit(solution)/shard_map/ppermute | solution.py:385
  148.9 2.7 %collective-permute-start.8 = (bf16[128,2048]{1,0:T(8,128)(2,1)}, bf16[128,2048]{1,0:T(8,128)(2,1)}, u32[]{:S(2)}, u32[]{:S(2)}) collective-permute-start(bf16[128,2048]{1,0:T(8,128)(2,1)} %collective-permute-done.3.refs_3_), channel_id=1, source_target_pairs={{0,1},{1,0},{2,3},{3,2},{4,5},{5,4},{6,7},{7,6},{8,9},{9,8},{10,11... | collective-permute-start | bytes 1572872 | tf_op jit(solution)/shard_map/ppermute | solution.py:385
  162.4 1.8 %collective-permute-start.11 = (bf16[256,512]{1,0:T(8,128)(2,1)}, bf16[256,512]{1,0:T(8,128)(2,1)S(1)}, u32[]{:S(2)}, u32[]{:S(2)}) collective-permute-start(bf16[256,512]{1,0:T(8,128)(2,1)} %get-tuple-element.18), channel_id=1, source_target_pairs={{0,1},{1,0},{2,3},{3,2},{4,5},{5,4},{6,7},{7,6},{8,9},{9,8},{10,11... | collective-permute-start | bytes 786440 | tf_op jit(solution)/shard_map/ppermute | solution.py:385
  164.2 0.7 copy-start.6
  (1 other events, 0.6 us)
Sparse Core Ops, SparseCore 0:
  17.1 123.2 all-gather.1
